TPU v7x, 256 devices: a whole 4x4x8 slice. The times are simulated.
256 devices in a mesh: dp: 8 (over y, core), label: 32 (over x, z).
Axes of the slice: x: 4, y: 4, z: 8, core: 2. Of those that a mesh axis runs over, the one named last changes fastest.
Arguments:
- queries: bfloat16 [32768, 512], P(('dp', 'label')), may hold values from -200 to 200
- shortlist: int32 [32768, 4], P(('dp', 'label')), may hold values from 0 to 511, all different within a row; in each aligned block of 128 rows (0 to 127, 128 to 255, ...) at most 2 rows name the same one
- slab_slot: int32 [512], replicated, may hold values from 0 to 511, each once
- top_target: int32 [32768], P(('dp', 'label')), may hold values from 0 to 2047
- leaf_target: int32 [32768], P(('dp', 'label')), may hold values from 0 to 127
- top_weight: bfloat16 [2048, 512], P('label'), may hold values from -0.25 to 0.25
- mid_weight: bfloat16 [512, 512], P(('dp', 'label')), may hold values from -0.25 to 0.25
- leaf_weight: bfloat16 [512, 128, 512], P(('dp', 'label')), may hold values from -0.25 to 0.25
Outputs:
- query_grad: float32 [32768, 512], P(('dp', 'label'))
- top_grad: float32 [2048, 512], P('label')
- mid_grad: float32 [512, 512], P(('dp', 'label'))
- leaf_grad: float32 [512, 128, 512], P(('dp', 'label'))
- losses: float32 [3, 32768], P(None, ('dp', 'label'))
Inputs may be any that keep to these rules, and one draw needn't show every extreme that they name: `shortlist`: each query names 4 different mid clusters; among the 128 queries of one device no cluster is named more than 2 times. Each cluster's mid and leaf rows are row slab_slot[c] of mid_weight and leaf_weight; every row is used once.
All inputs are finite; a program needn't handle non-finite values.
Results may differ from a plain program's by a relative error of at most 0.003.
Values may be sent and summed in bfloat16 or wider, within the bound.
A program may use at most 64 MiB of HBM per device.

v0:
```python
import jax
import jax.numpy as jnp
from jax import lax
from jax.experimental import pallas as pl
from jax.experimental.pallas import tpu as pltpu
from jax.sharding import PartitionSpec as P

D = 512
BLOCKS = 512
QD = 128
SHORT = 4
LEAF = 128
NZ = 8
NX = 4
NDP = 8
PLANE = NX * NDP
ROWS = 16
SLOTS = PLANE * ROWS
TABLE = 16
BLK = QD + TABLE
ORDER = (0, 1, 7, 2, 6, 3, 5, 4)
IDX = tuple(ORDER.index(o) for o in range(NZ))
NEG = -1e30
MESH = pl.DeviceIdType.MESH
F32 = jnp.float32
BF16 = jnp.bfloat16
NT = (((1,), (1,)), ((), ()))
TN = (((0,), (0,)), ((), ()))
NN = (((1,), (0,)), ((), ()))


def dot(a, b, dims):
    return lax.dot_general(a, b, dims, preferred_element_type=F32)


def split3(v):
    hi = v.astype(BF16)
    rest = v - hi.astype(F32)
    mid = rest.astype(BF16)
    low = (rest - mid.astype(F32)).astype(BF16)
    return hi, mid, low


def iota(shape, dim):
    return lax.broadcasted_iota(jnp.int32, shape, dim)


def kernel(
    blk_ref, leaf_ref, mid_ref, topw_ref,
    qg_ref, tg_ref, mg_ref, lg_ref, loss_ref,
    gq, xw, wext, oht, pk, rb, sk, ts, live_ref, info, cmsg, crecv, emsg, erecv, fmsg, frecv,
    stat, zstat, zlse, part, ob, pbk, tgs, tgr, losss, lossr, rsS, rsR,
    psend, precv, agsend, agrecv, rssend, rsrecv, zsend, zrecv, wsend, wrecv, osend, orecv,
):
    dp = lax.axis_index("dp")
    label = lax.axis_index("label")
    x = label // NZ
    z = label % NZ
    me = x * NDP + dp

    def plane_id(t):
        return (t % NDP, (t // NDP) * NZ + z)

    def z_id(d):
        return (dp, x * NZ + (z + d) % NZ)

    def x_id(d):
        return (dp, ((x + d) % NX) * NZ + z)

    def dp_id(d):
        return ((dp + d) % NDP, label)

    gq[0] = blk_ref[...]
    wext[0:256, :] = leaf_ref[...].reshape(256, D)
    wext[256:272, :] = jnp.concatenate(
        [mid_ref[...].astype(F32), jnp.zeros((14, D), F32)], axis=0
    ).astype(BF16)

    barrier = pltpu.get_barrier_semaphore()

    def greet(i, _):
        pl.semaphore_signal(barrier, inc=1, device_id=plane_id((me + i) % PLANE), device_id_type=MESH)
        return 0

    lax.fori_loop(1, PLANE, greet, 0)
    for d in range(1, NZ):
        pl.semaphore_signal(barrier, inc=1, device_id=z_id(d), device_id_type=MESH)
    pl.semaphore_wait(barrier, PLANE - 1 + NZ - 1)

    cuts = ((0, 80), (80, 64))

    def ag(direction, hop, chunk):
        start, length = cuts[chunk]
        if direction == 0:
            src, dst, to = IDX[(NZ - hop + 1) % NZ], IDX[NZ - hop], 1
        else:
            src, dst, to = IDX[hop - 1], IDX[hop], NZ - 1
        rows = pl.ds(start, length)
        return pltpu.make_async_remote_copy(
            src_ref=gq.at[src, rows], dst_ref=gq.at[dst, rows],
            send_sem=agsend.at[direction, hop - 1, chunk],
            recv_sem=agrecv.at[direction, hop - 1, chunk],
            device_id=z_id(to), device_id_type=MESH,
        )

    def flows(hop):
        return [(0, 0), (1, 1), (1, 0), (0, 1)] if hop < 4 else [(0, 0), (1, 1)]

    for direction, chunk in flows(1):
        ag(direction, 1, chunk).start()

    def wcopy(d):
        return pltpu.make_async_remote_copy(
            src_ref=topw_ref, dst_ref=xw.at[x], send_sem=wsend.at[d], recv_sem=wrecv.at[d],
            device_id=x_id(d), device_id_type=MESH,
        )

    def wwait(d):
        return pltpu.make_async_remote_copy(
            src_ref=topw_ref, dst_ref=xw.at[(x - d + NX) % NX], send_sem=wsend.at[d],
            recv_sem=wrecv.at[d], device_id=x_id(d), device_id_type=MESH,
        )

    for d in range(1, NX):
        wcopy(d).start()
    xw[x] = topw_ref[...]

    def plane_send(phase, source, target):
        def body(i, _):
            t = (me + i) % PLANE
            pltpu.make_async_remote_copy(
                src_ref=source(t), dst_ref=target(me), send_sem=psend.at[phase, i],
                recv_sem=precv.at[phase, i], device_id=plane_id(t), device_id_type=MESH,
            ).start()
            return 0

        lax.fori_loop(1, PLANE, body, 0)

    def plane_wait(phase, source, target, sent):
        def body(i, _):
            t = (me + i) % PLANE
            f = (me - i + PLANE) % PLANE
            copy = pltpu.make_async_remote_copy(
                src_ref=source(t), dst_ref=target(f), send_sem=psend.at[phase, i],
                recv_sem=precv.at[phase, i], device_id=plane_id(t), device_id_type=MESH,
            )
            if sent:
                copy.wait_send()
            else:
                copy.wait_recv()
            return 0

        lax.fori_loop(1, PLANE, body, 0)

    exchanges = {
        "rows0": (0, lambda t: pk.at[0, t], lambda f: rb.at[0, f]),
        "rows1": (1, lambda t: pk.at[1, t], lambda f: rb.at[1, f]),
        "code": (2, lambda t: cmsg.at[t // NDP], lambda f: crecv.at[f]),
        "ex1": (3, lambda t: emsg.at[t // NDP], lambda f: erecv.at[f]),
        "ex2": (4, lambda t: fmsg.at[t // NDP], lambda f: frecv.at[f]),
        "ret1": (5, lambda t: ob.at[1, t], lambda f: pbk.at[1, f]),
        "ret0": (6, lambda t: ob.at[0, t], lambda f: pbk.at[0, f]),
        "tg": (7, lambda t: tgs.at[t], lambda f: tgr.at[f]),
    }

    def send(name):
        plane_send(*exchanges[name])

    def arrived(name):
        plane_wait(*exchanges[name], False)

    def left(name):
        plane_wait(*exchanges[name], True)

    lane = iota((8, 128), 1)

    def regroup(received):
        groups = []
        for g in range(NX):
            out = jnp.zeros((8, 128), F32)
            for j in range(NDP):
                turned = pltpu.roll(received[g * NDP + j], ((j - dp + NDP) % NDP) * ROWS, axis=1)
                out = jnp.where(lane // ROWS == j, turned, out)
            groups.append(out)
        return jnp.concatenate(groups, axis=1)

    qid = iota((SLOTS, SLOTS), 0)

    def pack(s):
        ids = jnp.zeros((1, SLOTS), F32)
        first = jnp.zeros((1, SLOTS), F32)
        targets = []
        for o4 in range(4):
            table = gq[4 * s + o4, QD:BLK, :].astype(F32)
            row = jnp.sum(jnp.where(iota((TABLE, D), 0) == z, table, 0.0), axis=0, keepdims=True)
            ids = ids + jnp.where(row != 0.0, jnp.abs(row) + o4 * QD, 0.0)
            first = first + jnp.where(row < 0.0, 1.0, 0.0)
            targets.append(table[8:9, 0:QD])
            top = (table[8:9, QD : 2 * QD] * 16.0 + table[8:9, 2 * QD : 3 * QD]).astype(jnp.int32)
            here = ((top >> 6) & 7) == z
            place = ((top >> 9) << 6) + (top & 63)
            info[4 * s + o4 : 4 * s + o4 + 1, :] = jnp.where(here, place, -1)
        hot = jnp.where(qid == ids.astype(jnp.int32) - 1, 1.0, 0.0).astype(BF16)
        oht[s] = hot
        queries = gq[4 * s : 4 * s + 4, 0:QD, :].reshape(SLOTS, D)
        pk[s] = dot(hot, queries, TN).astype(BF16).reshape(PLANE, ROWS, D)
        wanted = jnp.broadcast_to(jnp.concatenate(targets, axis=1), (8, SLOTS)).astype(BF16)
        code = dot(wanted, hot, NN)[0:1, :]
        code = jnp.where(ids > 0.0, jnp.where(first > 0.0, code, -1.0), -2.0)
        live_ref[s : s + 1, :] = jnp.where(first > 0.0, 1.0, 0.0)
        for g in range(NX):
            cmsg[g, s : s + 1, :] = code[:, g * 128 : (g + 1) * 128]

    def top_scores(s):
        queries = gq[4 * s : 4 * s + 4, 0:QD, :].reshape(SLOTS, D)
        scores = dot(xw[...].reshape(256, D), queries, NT)
        ts[s] = scores
        largest = jnp.max(scores, axis=0, keepdims=True)
        total = largest + jnp.log(jnp.sum(jnp.exp(scores - largest), axis=0, keepdims=True))
        for o4 in range(4):
            o = ORDER[4 * s + o4]
            stat[2, o : o + 1, :] = total[:, o4 * 128 : (o4 + 1) * 128]

    def own_rows(s):
        rb[s, me] = pk[s, me]

    for hop in (2, 3):
        for direction, chunk in flows(hop):
            ag(direction, hop - 1, chunk).wait_recv()
            ag(direction, hop, chunk).start()
    pack(0)
    send("rows0")
    own_rows(0)
    for direction, chunk in flows(4):
        ag(direction, 3, chunk).wait_recv()
        ag(direction, 4, chunk).start()
    for d in range(1, NX):
        wwait(d).wait_recv()
    top_scores(0)
    for direction, chunk in ((1, 0), (0, 1)):
        ag(direction, 3, chunk).wait_recv()
    for direction, chunk in flows(4):
        ag(direction, 4, chunk).wait_recv()
    for g in range(NX):
        cmsg[g, 2:8, :] = jnp.zeros((6, 128), F32)
    pack(1)
    send("rows1")
    send("code")
    own_rows(1)
    crecv[me] = cmsg[x]
    top_scores(1)

    odd = (iota((1, SLOTS), 1) >> 3) & 1

    def holder_scores(s):
        scores = dot(wext[...], rb[s].reshape(SLOTS, D), NT)
        sk[s, 0:LEAF, :] = jnp.where(odd == 0, scores[0:LEAF], scores[LEAF : 2 * LEAF])
        sk[s, LEAF : LEAF + 8, :] = jnp.broadcast_to(
            jnp.where(odd == 0, scores[256:257], scores[257:258]), (8, SLOTS)
        )

    arrived("rows0")
    holder_scores(0)
    arrived("rows1")
    holder_scores(1)
    arrived("code")
    codes = regroup(crecv)
    label_row = iota((LEAF, SLOTS), 0)
    for s in range(2):
        chosen = sk[s, 0:LEAF, :]
        code = codes[s : s + 1, :].astype(jnp.int32)
        largest = jnp.max(chosen, axis=0, keepdims=True)
        total = largest + jnp.log(jnp.sum(jnp.exp(chosen - largest), axis=0, keepdims=True))
        target = jnp.sum(jnp.where(label_row == code, chosen, 0.0), axis=0, keepdims=True)
        middle = sk[s, LEAF : LEAF + 1, :]
        for g in range(NX):
            span = slice(g * 128, (g + 1) * 128)
            emsg[g, 4 * s : 4 * s + 1, :] = total[:, span]
            emsg[g, 4 * s + 1 : 4 * s + 2, :] = middle[:, span]
            emsg[g, 4 * s + 2 : 4 * s + 3, :] = target[:, span]
            emsg[g, 4 * s + 3 : 4 * s + 4, :] = target[:, span]
    send("ex1")
    erecv[me] = emsg[x]
    arrived("ex1")
    pairs = regroup(erecv)

    eye = iota((QD, QD), 0) == iota((QD, QD), 1)
    for s in range(2):
        hot = oht[s].astype(F32) > 0.5
        for which in range(2):
            values = jnp.where(hot, pairs[4 * s + which : 4 * s + which + 1, :], NEG)
            largest = jnp.max(values, axis=1, keepdims=True)
            total = largest + jnp.log(jnp.sum(jnp.exp(values - largest), axis=1, keepdims=True))
            for o4 in range(4):
                o = ORDER[4 * s + o4]
                piece = jnp.where(eye, total[o4 * QD : (o4 + 1) * QD], 0.0)
                stat[which, o : o + 1, :] = jnp.sum(piece, axis=0, keepdims=True)

    def zcopy(d):
        return pltpu.make_async_remote_copy(
            src_ref=stat, dst_ref=zstat.at[d], send_sem=zsend.at[0, d], recv_sem=zrecv.at[0, d],
            device_id=z_id(d), device_id_type=MESH,
        )

    for d in range(1, NZ):
        zcopy(d).start()
    for d in range(1, NZ):
        zcopy(d).wait_recv()
    for which in range(3):
        views = [stat[which]]
        for d in range(1, NZ):
            views.append(pltpu.roll(zstat[d, which], NZ - d, axis=0))
        largest = views[0]
        for view in views[1:]:
            largest = jnp.maximum(largest, view)
        total = jnp.zeros((NZ, 128), F32)
        for view in views:
            total = total + jnp.exp(view - largest)
        zlse[which] = largest + jnp.log(total)

    def query_row(which, s):
        return jnp.concatenate([zlse[which, ORDER[4 * s + o4] : ORDER[4 * s + o4] + 1, :] for o4 in range(4)], axis=1)

    slot_values = []
    for s in range(2):
        pieces = split3(query_row(0, s)) + split3(query_row(1, s))
        pieces = [piece.astype(F32) for piece in pieces] + [jnp.zeros((10, SLOTS), F32)]
        rows = dot(jnp.concatenate(pieces, axis=0).astype(BF16), oht[s], NN)
        leaf_slot = rows[0:1] + rows[1:2] + rows[2:3]
        mid_slot = rows[3:4] + rows[4:5] + rows[5:6]
        slot_values.append((leaf_slot, mid_slot))
        for g in range(NX):
            span = slice(g * 128, (g + 1) * 128)
            fmsg[g, 4 * s : 4 * s + 1, :] = leaf_slot[:, span]
            fmsg[g, 4 * s + 1 : 4 * s + 2, :] = mid_slot[:, span]
            fmsg[g, 4 * s + 2 : 4 * s + 3, :] = mid_slot[:, span]
            fmsg[g, 4 * s + 3 : 4 * s + 4, :] = mid_slot[:, span]
    send("ex2")
    frecv[me] = fmsg[x]

    weights = xw[...].reshape(256, D)
    class_row = iota((256, SLOTS), 0)
    grad = jnp.zeros((256, D), F32)
    for s in range(2):
        scores = ts[s]
        totals = query_row(2, s)
        place = jnp.concatenate([info[4 * s + o4 : 4 * s + o4 + 1, :] for o4 in range(4)], axis=1)
        hit = class_row == place
        delta = (jnp.exp(scores - totals) - jnp.where(hit, 1.0, 0.0)).astype(BF16)
        score = jnp.sum(jnp.where(hit, scores, 0.0), axis=0, keepdims=True)
        top_loss = jnp.where(place >= 0, totals - score, 0.0)
        grad = grad + dot(delta, gq[4 * s : 4 * s + 4, 0:QD, :].reshape(SLOTS, D), NN)
        part[s] = dot(delta, weights, TN)
        leaf_slot, mid_slot = slot_values[s]
        first = live_ref[s : s + 1, :] > 0.5
        leaf_loss = jnp.where(first, leaf_slot - pairs[4 * s + 2 : 4 * s + 3, :], 0.0)
        mid_loss = jnp.where(first, mid_slot - pairs[4 * s + 1 : 4 * s + 2, :], 0.0)
        pieces = split3(leaf_loss) + split3(mid_loss)
        pieces = [piece.astype(F32) for piece in pieces] + [jnp.zeros((10, SLOTS), F32)]
        rows = dot(jnp.concatenate(pieces, axis=0).astype(BF16), oht[s], NT)
        leaf_query = rows[0:1] + rows[1:2] + rows[2:3]
        mid_query = rows[3:4] + rows[4:5] + rows[5:6]
        for o4 in range(4):
            o = ORDER[4 * s + o4]
            span = slice(o4 * 128, (o4 + 1) * 128)
            losss[o] = jnp.concatenate(
                [top_loss[:, span], mid_query[:, span], leaf_query[:, span], jnp.zeros((5, 128), F32)],
                axis=0,
            )
    tgs[...] = grad.reshape(PLANE, 8, D)

    def losscopy(o):
        return pltpu.make_async_remote_copy(
            src_ref=losss.at[o], dst_ref=lossr.at[o], send_sem=zsend.at[1, o],
            recv_sem=zrecv.at[1, o], device_id=z_id(o), device_id_type=MESH,
        )

    arrived("ex2")
    scalars = regroup(frecv)
    deltas = []
    for s in (1, 0):
        code = codes[s : s + 1, :].astype(jnp.int32)
        live = code > -2
        hit = jnp.where(label_row == code, 1.0, 0.0)
        delta = jnp.where(live, jnp.exp(sk[s, 0:LEAF, :] - scalars[4 * s : 4 * s + 1, :]) - hit, 0.0)
        middle = jnp.exp(sk[s, LEAF : LEAF + 1, :] - scalars[4 * s + 1 : 4 * s + 2, :])
        middle = jnp.where(live, middle - jnp.where(code >= 0, 1.0, 0.0), 0.0)
        even = odd == 0
        whole = jnp.concatenate(
            [
                jnp.where(even, delta, 0.0), jnp.where(even, 0.0, delta),
                jnp.where(even, middle, 0.0), jnp.where(even, 0.0, middle),
                jnp.zeros((14, SLOTS), F32),
            ],
            axis=0,
        ).astype(BF16)
        deltas.append(whole)
        ob[s] = dot(whole, wext[...], TN).astype(BF16).reshape(PLANE, ROWS, D)
        send("ret1" if s else "ret0")
        pbk[s, me] = ob[s, me]
    for o in range(1, NZ):
        losscopy(o).start()
    send("tg")
    tgr[me] = tgs[me]
    grads = dot(deltas[0], rb[1].reshape(SLOTS, D), NN) + dot(deltas[1], rb[0].reshape(SLOTS, D), NN)
    lg_ref[...] = grads[0:256].reshape(2, LEAF, D)
    mg_ref[...] = grads[256:258]

    halves = (pl.ds(0, 64), pl.ds(64, 64))

    def rs(direction, hop, chunk):
        return pltpu.make_async_remote_copy(
            src_ref=rsS.at[direction, hop, halves[chunk]],
            dst_ref=rsR.at[direction, hop, halves[chunk]],
            send_sem=rssend.at[direction, hop, chunk], recv_sem=rsrecv.at[direction, hop, chunk],
            device_id=z_id(1 if direction == 0 else NZ - 1), device_id_type=MESH,
        )

    def rs_step(direction, hop, chunk):
        o = 4 - hop if direction == 0 else 4 + hop
        index = IDX[o]
        rows = pl.ds((index % 4) * QD + chunk * 64, 64)
        value = part[index // 4, rows, :]
        if hop > 1 or (hop == 1 and chunk == direction):
            rs(direction, hop - 1, chunk).wait_recv()
            value = value + rsR[direction, hop - 1, halves[chunk], :].astype(F32)
        rsS[direction, hop, halves[chunk], :] = value.astype(BF16)
        rs(direction, hop, chunk).start()

    for s in (1, 0):
        arrived("ret1" if s else "ret0")
        part[s] = part[s] + dot(oht[s], pbk[s].reshape(SLOTS, D), NN)
        if s:
            for direction in range(2):
                rs_step(direction, 0, direction)
            for direction in range(2):
                rs_step(direction, 1, 1 - direction)
            rs_step(0, 1, 0)
            rs_step(1, 1, 1)
            rs_step(1, 2, 0)
            rs_step(1, 2, 1)
    rs_step(0, 2, 1)
    rs_step(0, 2, 0)

    arrived("tg")
    tg_sum = tgr[0]
    for f in range(1, PLANE):
        tg_sum = tg_sum + tgr[f]
    tg_ref[pl.ds(pl.multiple_of(dp * 8, 8), 8), :] = tg_sum

    def tgcopy(d, who):
        rows = pl.ds(pl.multiple_of(who * 8, 8), 8)
        return pltpu.make_async_remote_copy(
            src_ref=tg_ref.at[rows], dst_ref=tg_ref.at[rows], send_sem=osend.at[d],
            recv_sem=orecv.at[d], device_id=dp_id(d), device_id_type=MESH,
        )

    for d in range(1, NDP):
        tgcopy(d, dp).start()

    for direction in range(2):
        for chunk in range(2):
            rs_step(direction, 3, chunk)

    for o in range(1, NZ):
        losscopy(o).wait_recv()
    losses = losss[0]
    for o in range(1, NZ):
        losses = losses + lossr[o]
    loss_ref[...] = losses[0:3]

    for direction in range(2):
        for chunk in range(2):
            rs(direction, 3, chunk).wait_recv()
    qg_ref[...] = part[0, 0:QD, :] + rsR[0, 3].astype(F32) + rsR[1, 3].astype(F32)

    for d in range(1, NDP):
        tgcopy(d, (dp - d + NDP) % NDP).wait_recv()

    for hop in range(1, 5):
        for direction, chunk in flows(hop):
            ag(direction, hop, chunk).wait_send()
    for d in range(1, NX):
        wcopy(d).wait_send()
    for name in exchanges:
        left(name)
    for d in range(1, NZ):
        zcopy(d).wait_send()
        losscopy(d).wait_send()
    for hop in range(4):
        for direction in range(2):
            for chunk in range(2):
                if hop > 0 or chunk == direction:
                    rs(direction, hop, chunk).wait_send()
    for d in range(1, NDP):
        tgcopy(d, dp).wait_send()


def build_block(queries, shortlist, slab_slot, top_target, leaf_target):
    z = lax.axis_index("label") % NZ
    count = QD * SHORT
    named = shortlist.reshape(-1)
    cluster = jnp.arange(BLOCKS, dtype=jnp.int32)
    position = jnp.sum(jnp.where(named[:, None] == cluster[None, :], slab_slot[None, :], 0), axis=1)
    pair = jnp.arange(count, dtype=jnp.int32)
    earlier = (position[:, None] == position[None, :]) & (pair[None, :] < pair[:, None])
    rank = jnp.sum(earlier.astype(jnp.int32), axis=1)
    k, flat = position % 2, position // 2
    holder_dp, holder_x, holder_z = flat // 32, (flat % 32) // NZ, flat % NZ
    offset = (z - holder_z + NZ) % NZ
    index = jnp.zeros_like(offset)
    for o in range(NZ):
        index = jnp.where(offset == o, IDX[o], index)
    lane = (holder_x * NDP + holder_dp) * ROWS + k * 8 + (index % 4) * 2 + rank
    query = pair // SHORT
    sign = jnp.where(pair % SHORT == 0, -1, 1)
    value = (sign * (query + 1)).astype(BF16)
    planes = jnp.arange(NZ, dtype=jnp.int32)
    left = jnp.where(holder_z[:, None] == planes[None, :], value[:, None], jnp.zeros((), BF16))
    right = (lane[:, None] == jnp.arange(SLOTS, dtype=jnp.int32)[None, :]).astype(BF16)
    table = lax.dot_general(left, right, TN, preferred_element_type=F32).astype(BF16)
    row = jnp.concatenate([leaf_target, top_target // 16, top_target % 16, jnp.zeros_like(leaf_target)])
    row = row.astype(BF16)[None, :]
    return jnp.concatenate([queries, table, row, jnp.zeros((TABLE - NZ - 1, D), BF16)], axis=0)


def per_device(queries, shortlist, slab_slot, top_target, leaf_target, top_weight, mid_weight, leaf_weight):
    block = build_block(queries, shortlist, slab_slot, top_target, leaf_target)
    vmem = pl.BlockSpec(memory_space=pltpu.VMEM)
    sem = pltpu.SemaphoreType.DMA
    scratch = [
        pltpu.VMEM((NZ, BLK, D), BF16),
        pltpu.VMEM((NX, 64, D), BF16),
        pltpu.VMEM((272, D), BF16),
        pltpu.VMEM((2, SLOTS, SLOTS), BF16),
        pltpu.VMEM((2, PLANE, ROWS, D), BF16),
        pltpu.VMEM((2, PLANE, ROWS, D), BF16),
        pltpu.VMEM((2, LEAF + 8, SLOTS), F32),
        pltpu.VMEM((2, 256, SLOTS), F32),
        pltpu.VMEM((8, SLOTS), F32),
        pltpu.VMEM((NZ, 128), jnp.int32),
        pltpu.VMEM((NX, 8, 128), F32),
        pltpu.VMEM((PLANE, 8, 128), F32),
        pltpu.VMEM((NX, 8, 128), F32),
        pltpu.VMEM((PLANE, 8, 128), F32),
        pltpu.VMEM((NX, 8, 128), F32),
        pltpu.VMEM((PLANE, 8, 128), F32),
        pltpu.VMEM((3, NZ, 128), F32),
        pltpu.VMEM((NZ, 3, NZ, 128), F32),
        pltpu.VMEM((3, NZ, 128), F32),
        pltpu.VMEM((2, SLOTS, D), F32),
        pltpu.VMEM((2, PLANE, ROWS, D), BF16),
        pltpu.VMEM((2, PLANE, ROWS, D), BF16),
        pltpu.VMEM((PLANE, 8, D), F32),
        pltpu.VMEM((PLANE, 8, D), F32),
        pltpu.VMEM((NZ, 8, 128), F32),
        pltpu.VMEM((NZ, 8, 128), F32),
        pltpu.VMEM((2, 4, QD, D), BF16),
        pltpu.VMEM((2, 4, QD, D), BF16),
        sem((8, PLANE)), sem((8, PLANE)),
        sem((2, 4, 2)), sem((2, 4, 2)),
        sem((2, 4, 2)), sem((2, 4, 2)),
        sem((2, NZ)), sem((2, NZ)),
        sem((NX,)), sem((NX,)),
        sem((NDP,)), sem((NDP,)),
    ]
    query_grad, top_grad, mid_grad, leaf_grad, losses = pl.pallas_call(
        kernel,
        out_shape=(
            jax.ShapeDtypeStruct((QD, D), F32),
            jax.ShapeDtypeStruct((64, D), F32),
            jax.ShapeDtypeStruct((2, D), F32),
            jax.ShapeDtypeStruct((2, LEAF, D), F32),
            jax.ShapeDtypeStruct((3, QD), F32),
        ),
        in_specs=[vmem] * 4,
        out_specs=(vmem,) * 5,
        scratch_shapes=scratch,
        compiler_params=pltpu.CompilerParams(
            collective_id=0, has_side_effects=True, vmem_limit_bytes=48 << 20
        ),
    )(block, leaf_weight, mid_weight, top_weight)
    return query_grad, top_grad, mid_grad, leaf_grad, losses


def solution(mesh):
    both = ("dp", "label")
    in_specs = (
        P(both, None), P(both, None), P(), P(both), P(both),
        P("label", None), P(both, None), P(both, None, None),
    )
    out_specs = (
        P(both, None), P("label", None), P(both, None), P(both, None, None), P(None, both),
    )
    return jax.shard_map(
        per_device, mesh=mesh, in_specs=in_specs, out_specs=out_specs, check_vma=False
    )
```

profile of v0, /device:TPU:1, one launch (start us, length us, event | category | flops | bytes accessed | tf_op | source)
XLA Modules:
  0.0 102.2 jit_solution(3741213068792974981)
XLA Ops:
  0.7 0.0 copy-start.6
  0.7 0.0 copy-start.7
  0.7 0.1 pad.6.clone
  0.8 0.6 copy-done.6
  1.3 0.0 copy-done.7
  1.3 0.0 copy-start.4
  1.4 0.7 copy-done.4
  2.0 0.1 copy.14
  2.1 0.1 eq.131
  2.3 0.6 copy-done.5
  2.8 0.2 select_reduce_fusion
  3.1 0.3 convert_reduce_fusion
  3.4 0.0 copy-start.3
  3.4 0.5 convolution_convert_fusion
  3.9 0.4 copy-done.3
  4.3 0.1 maximum_maximum_fusion.blk_ref
  4.4 0.5 copy-done
  4.8 0.1 copy-done.2
  5.0 93.9 %shard_map.119 = (f32[128,512]{1,0:T(8,128)S(1)}, f32[64,512]{1,0:T(8,128)S(1)}, f32[2,512]{1,0:T(2,128)S(1)}, f32[2,128,512]{2,1,0:T(8,128)S(1)}, f32[3,128]{1,0:T(4,128)S(1)}) custom-call(bf16[144,512]{1,0:T(8,128)(2,1)S(1)} %maximum_maximum_fusion.blk_ref, bf16[2,128,512]{2,1,0:T(8,128)(2,1)S(1)} %copy-done, bf16[2,512]{1,0:T(2,128)(2,1)S(1)} %copy-done.2, ...), custom_call_target="tpu_custom_call" | custom-call | tf_op jit(solution)/shard_map/pallas_call | solution.py:567
  98.8 0.7 copy.20
  99.6 0.7 copy.21
  100.2 0.6 copy.22
  100.8 0.8 copy.23
  101.6 0.6 copy.24
  (9 shorter events, 0.1 us)
Async XLA Ops:
  0.7 0.7 copy-start.6
  0.7 0.7 copy-start.7
  1.3 0.7 copy-start.4
  2.1 0.7 copy-start.5
  3.4 0.9 copy-start.3
  3.4 1.0 copy-start.1
  3.9 1.0 copy-start
  4.3 0.7 copy-start.2
where the time goes:
time: 102 us
  Pallas kernels  93.9 us (92%)
  local copies, waits for them, and re-layouts  6.46 us (6%)
    pallas_call x1, Pallas kernels, per_device(): pl.pallas_call(kernel, out_shape=(jax.ShapeDtypeStruct((QD, D), F32), jax...  93.9 us
    unnamed x22, local copies, waits for them, and re-layouts  6.28 us

commit v1 on v0

v1 whole, which is shorter than its diff:
```python
import jax
import jax.numpy as jnp
from jax import lax
from jax.experimental import pallas as pl
from jax.experimental.pallas import tpu as pltpu
from jax.sharding import PartitionSpec as P

D = 512
BLOCKS = 512
QD = 128
SHORT = 4
LEAF = 128
NZ = 8
NX = 4
NDP = 8
PLANE = NX * NDP
ROWS = 16
SLOTS = PLANE * ROWS
ORDER = (0, 1, 7, 2, 6, 3, 5, 4)
IDX = tuple(ORDER.index(o) for o in range(NZ))
NEG = -1e30
MESH = pl.DeviceIdType.MESH
F32 = jnp.float32
BF16 = jnp.bfloat16
NT = (((1,), (1,)), ((), ()))
TN = (((0,), (0,)), ((), ()))
NN = (((1,), (0,)), ((), ()))


def dot(a, b, dims):
    return lax.dot_general(a, b, dims, preferred_element_type=F32)


def split3(v):
    hi = v.astype(BF16)
    rest = v - hi.astype(F32)
    mid = rest.astype(BF16)
    low = (rest - mid.astype(F32)).astype(BF16)
    return hi, mid, low


def iota(shape, dim):
    return lax.broadcasted_iota(jnp.int32, shape, dim)


def kernel(
    query_in, short_in, slab_in, target_in, leaftarget_in, leaf_in, mid_in, topw_in,
    qg_out, tg_out, mg_out, lg_out, loss_out,
    gq, short_ref, slab_ref, target_ref, leaftarget_ref, mid_ref, tab, tabs,
    xw, wext, oht, slotinfo, pk, rb, sk, ts, cmsg, crecv, emsg, erecv, fmsg, frecv,
    stat, zstat, zlse, tstat, ztop, part, ob, pbk, tgs, tgr, losss, lossr, rsS, rsR,
    qg_ref, tg_ref, mg_ref, lg_ref, loss_ref,
    psend, precv, agsend, agrecv, rssend, rsrecv, zsend, zrecv, wsend, wrecv, osend, orecv, insem, outsem,
):
    dp = lax.axis_index("dp")
    label = lax.axis_index("label")
    x = label // NZ
    z = lax.rem(label, NZ)
    me = x * NDP + dp

    def partner(i):
        tx, td = lax.rem(x + i // NDP, NX), lax.rem(dp + i % NDP, NDP)
        return tx, td

    def plane_id(i):
        tx, td = partner(i)
        return (td, tx * NZ + z)

    def z_id(d):
        return (dp, x * NZ + lax.rem(z + d, NZ))

    def x_id(d):
        return (dp, lax.rem(x + d, NX) * NZ + z)

    def dp_id(d):
        return (lax.rem(dp + d, NDP), label)

    pending = []

    def finish():
        for wait in pending:
            wait()

    barrier = pltpu.get_barrier_semaphore()
    for i in range(1, PLANE):
        pl.semaphore_signal(barrier, inc=1, device_id=plane_id(i), device_id_type=MESH)
    for d in range(1, NZ):
        pl.semaphore_signal(barrier, inc=1, device_id=z_id(d), device_id_type=MESH)

    loads = [
        pltpu.make_async_copy(a, b, insem.at[n])
        for n, (a, b) in enumerate((
            (query_in, gq.at[0]), (short_in, short_ref), (slab_in, slab_ref), (target_in, target_ref),
            (leaftarget_in, leaftarget_ref), (topw_in, xw.at[x]), (mid_in, mid_ref),
            (leaf_in.at[0], wext.at[pl.ds(0, LEAF)]), (leaf_in.at[1], wext.at[pl.ds(LEAF, LEAF)]),
        ))
    ]
    for load in loads:
        load.start()
    loads[0].wait()
    loads[5].wait()
    pl.semaphore_wait(barrier, PLANE - 1 + NZ - 1)

    cuts = ((0, 64), (64, 64))

    def ag(direction, hop, chunk):
        start, length = cuts[chunk]
        if direction == 0:
            src, dst, to = IDX[(NZ - hop + 1) % NZ], IDX[NZ - hop], 1
        else:
            src, dst, to = IDX[hop - 1], IDX[hop], NZ - 1
        rows = pl.ds(start, length)
        return pltpu.make_async_remote_copy(
            src_ref=gq.at[src, rows], dst_ref=gq.at[dst, rows],
            send_sem=agsend.at[direction, hop - 1, chunk],
            recv_sem=agrecv.at[direction, hop - 1, chunk],
            device_id=z_id(to), device_id_type=MESH,
        )

    def ag_start(direction, hop, chunk):
        copy = ag(direction, hop, chunk)
        copy.start()
        pending.append(copy.wait_send)

    def flows(hop):
        return [(0, 0), (1, 1), (1, 0), (0, 1)] if hop < 4 else [(0, 0), (1, 1)]

    for direction, chunk in flows(1):
        ag_start(direction, 1, chunk)

    def wcopy(d, owner):
        return pltpu.make_async_remote_copy(
            src_ref=xw.at[owner], dst_ref=xw.at[owner], send_sem=wsend.at[d], recv_sem=wrecv.at[d],
            device_id=x_id(d), device_id_type=MESH,
        )

    for d in range(1, NX):
        wcopy(d, x).start()
        pending.append(wcopy(d, x).wait_send)

    def remote(phase, source, target, to):
        return pltpu.make_async_remote_copy(
            src_ref=source, dst_ref=target, send_sem=psend.at[phase], recv_sem=precv.at[phase],
            device_id=to, device_id_type=MESH,
        )

    span31 = pl.ds(0, PLANE - 1)
    exchanges = {
        "rows0": (0, lambda tx, td: pk.at[0, tx * NDP + td], rb.at[0]),
        "rows1": (1, lambda tx, td: pk.at[1, tx * NDP + td], rb.at[1]),
        "code": (2, lambda tx, td: cmsg.at[tx], crecv),
        "ex1": (3, lambda tx, td: emsg.at[tx], erecv),
        "ex2": (4, lambda tx, td: fmsg.at[tx], frecv),
        "ret1": (5, lambda tx, td: ob.at[1, tx * NDP + td], pbk.at[1]),
        "ret0": (6, lambda tx, td: ob.at[0, tx * NDP + td], pbk.at[0]),
        "tg": (7, lambda tx, td: tgs.at[tx * NDP + td], tgr),
    }

    def whole(name):
        phase, _, target = exchanges[name]
        return remote(phase, target.at[span31], target.at[span31], plane_id(1))

    def send(name):
        phase, source, target = exchanges[name]
        for i in range(1, PLANE):
            remote(phase, source(*partner(i)), target.at[me], plane_id(i)).start()
        pending.append(whole(name).wait_send)

    def arrived(name):
        whole(name).wait_recv()

    lane = iota((8, 128), 1)

    def regroup(received):
        groups = []
        for g in range(NX):
            out = jnp.zeros((8, 128), F32)
            for j in range(NDP):
                turned = pltpu.roll(received[g * NDP + j], lax.rem(j - dp + NDP, NDP) * ROWS, axis=1)
                out = jnp.where(lane // ROWS == j, turned, out)
            groups.append(out)
        return jnp.concatenate(groups, axis=1)

    for load in loads[1:5]:
        load.wait()
    wide = iota((QD, SLOTS), 1)
    narrow = iota((QD, QD), 1)
    query_col = iota((QD, 1), 0)
    eye = iota((QD, QD), 0) == narrow
    slab = slab_ref[...].astype(F32)
    lower = jnp.where(iota((QD, QD), 1) < iota((QD, QD), 0), 1.0, 0.0).astype(BF16)
    base = jnp.zeros((1, SLOTS), F32)
    table = jnp.zeros((QD, QD), F32)
    for j in range(SHORT):
        named = jnp.sum(jnp.where(eye, short_ref[j : j + 1, :].astype(F32), 0.0), axis=1, keepdims=True).astype(jnp.int32)
        position = jnp.sum(jnp.where(wide == named, slab, 0.0), axis=1, keepdims=True).astype(jnp.int32)
        taken = wide == position
        ones = jnp.where(taken, 1.0, 0.0)
        before = dot(lower, ones.astype(BF16), NN) + base
        base = base + jnp.sum(ones, axis=0, keepdims=True)
        rank = jnp.sum(jnp.where(taken, before, 0.0), axis=1, keepdims=True).astype(jnp.int32)
        holder = position >> 1
        holder_z, holder_x, holder_dp = holder & 7, (holder >> 3) & 3, holder >> 5
        offset = (z - holder_z + NZ) & 7
        index = jnp.zeros((QD, 1), jnp.int32)
        for o in range(NZ):
            index = jnp.where(offset == o, IDX[o], index)
        place = holder_dp * ROWS + (position & 1) * 8 + (index & 3) * 2 + rank
        row = holder_z * NX + holder_x
        left = jnp.where(narrow == row, (query_col + 1).astype(F32), jnp.where(narrow == row + 32, j * 128.0, 0.0))
        right = jnp.where(narrow == place, 1.0, 0.0)
        table = table + dot(left.astype(BF16), right.astype(BF16), TN)
    table = table[0:32] + table[32:64]
    for p in range(NZ):
        tab[p, 0:4, :] = table[4 * p : 4 * p + 4]
        tab[p, 4:5, :] = leaftarget_ref[...].astype(F32)
        tab[p, 5:6, :] = target_ref[...].astype(F32)
        tab[p, 6:8, :] = jnp.zeros((2, 128), F32)

    def tabcopy(d):
        return pltpu.make_async_remote_copy(
            src_ref=tab.at[lax.rem(z + d, NZ)], dst_ref=tabs.at[IDX[NZ - d]], send_sem=zsend.at[2, d],
            recv_sem=zrecv.at[2, d], device_id=z_id(d), device_id_type=MESH,
        )

    for d in range(1, NZ):
        tabcopy(d).start()
        pending.append(tabcopy(d).wait_send)
    tabs[0] = tab[z]

    qid = iota((SLOTS, SLOTS), 0)

    def pack(s):
        ids = jnp.zeros((4, 128), jnp.int32)
        order = jnp.zeros((4, 128), jnp.int32)
        targets = []
        for o4 in range(4):
            tile = tabs[4 * s + o4].astype(jnp.int32)
            value = tile[0:4]
            ids = ids + jnp.where(value > 0, ((value - 1) & 127) + o4 * QD + 1, 0)
            order = order + jnp.where(value > 0, (value - 1) >> 7, 0)
            targets.append(tile[4:5].astype(F32))
        ids = jnp.concatenate([ids[g : g + 1] for g in range(NX)], axis=1)
        order = jnp.concatenate([order[g : g + 1] for g in range(NX)], axis=1)
        live = ids > 0
        hot = jnp.where(qid == ids - 1, 1.0, 0.0).astype(BF16)
        oht[s] = hot
        queries = gq[4 * s : 4 * s + 4].reshape(SLOTS, D)
        pk[s] = dot(hot, queries, TN).astype(BF16).reshape(PLANE, ROWS, D)
        slotinfo[s : s + 1, :] = jnp.where(live, order, -1)
        wanted = jnp.broadcast_to(jnp.concatenate(targets, axis=1), (8, SLOTS)).astype(BF16)
        code = dot(wanted, hot, NN)[0:1, :]
        code = jnp.where(live, jnp.where(order == 0, code, -1.0), -2.0)
        for g in range(NX):
            cmsg[g, s : s + 1, :] = code[:, g * 128 : (g + 1) * 128]

    def top_scores(s):
        queries = gq[4 * s : 4 * s + 4].reshape(SLOTS, D)
        scores = dot(xw[...].reshape(256, D), queries, NT)
        ts[s] = scores
        largest = jnp.max(scores, axis=0, keepdims=True)
        total = largest + jnp.log(jnp.sum(jnp.exp(scores - largest), axis=0, keepdims=True))
        for o4 in range(4):
            o = ORDER[4 * s + o4]
            tstat[o : o + 1, :] = total[:, o4 * 128 : (o4 + 1) * 128]

    for hop in (2, 3):
        for direction, chunk in flows(hop):
            ag(direction, hop - 1, chunk).wait_recv()
            ag_start(direction, hop, chunk)
    for d in range(1, NZ):
        tabcopy(d).wait_recv()
    pack(0)
    send("rows0")
    rb[0, me] = pk[0, me]
    for direction, chunk in flows(4):
        ag(direction, 3, chunk).wait_recv()
        ag_start(direction, 4, chunk)
    for d in range(1, NX):
        wcopy(d, lax.rem(x - d + NX, NX)).wait_recv()
    for load in loads[6:9]:
        load.wait()
    wext[256:272, :] = jnp.concatenate([mid_ref[...].astype(F32), jnp.zeros((14, D), F32)], axis=0).astype(BF16)
    for g in range(NX):
        cmsg[g, 2:8, :] = jnp.zeros((6, 128), F32)
    top_scores(0)
    for direction, chunk in ((1, 0), (0, 1)):
        ag(direction, 3, chunk).wait_recv()
    for direction, chunk in flows(4):
        ag(direction, 4, chunk).wait_recv()
    pack(1)
    send("rows1")
    send("code")
    rb[1, me] = pk[1, me]
    crecv[me] = cmsg[x]
    top_scores(1)

    def zshare(slot, source, target, d):
        return pltpu.make_async_remote_copy(
            src_ref=source, dst_ref=target.at[d], send_sem=zsend.at[slot, d], recv_sem=zrecv.at[slot, d],
            device_id=z_id(d), device_id_type=MESH,
        )

    def share(slot, source, target):
        for d in range(1, NZ):
            zshare(slot, source, target, d).start()
            pending.append(zshare(slot, source, target, d).wait_send)

    def shared(slot, source, target):
        for d in range(1, NZ):
            zshare(slot, source, target, d).wait_recv()

    def joined(own, views):
        views = [own] + [pltpu.roll(view, NZ - d, axis=0) for d, view in views]
        largest = views[0]
        for view in views[1:]:
            largest = jnp.maximum(largest, view)
        total = jnp.zeros((NZ, 128), F32)
        for view in views:
            total = total + jnp.exp(view - largest)
        return largest + jnp.log(total)

    share(3, tstat, ztop)

    odd = (iota((1, SLOTS), 1) >> 3) & 1

    def holder_scores(s):
        scores = dot(wext[...], rb[s].reshape(SLOTS, D), NT)
        sk[s, 0:LEAF, :] = jnp.where(odd == 0, scores[0:LEAF], scores[LEAF : 2 * LEAF])
        sk[s, LEAF : LEAF + 8, :] = jnp.broadcast_to(
            jnp.where(odd == 0, scores[256:257], scores[257:258]), (8, SLOTS)
        )
        chosen = sk[s, 0:LEAF, :]
        largest = jnp.max(chosen, axis=0, keepdims=True)
        total = largest + jnp.log(jnp.sum(jnp.exp(chosen - largest), axis=0, keepdims=True))
        middle = sk[s, LEAF : LEAF + 1, :]
        for g in range(NX):
            span = slice(g * 128, (g + 1) * 128)
            emsg[g, 4 * s : 4 * s + 1, :] = total[:, span]
            emsg[g, 4 * s + 1 : 4 * s + 2, :] = middle[:, span]

    arrived("rows0")
    holder_scores(0)
    arrived("rows1")
    holder_scores(1)
    arrived("code")
    codes = regroup(crecv)
    label_row = iota((LEAF, SLOTS), 0)
    for s in range(2):
        code = codes[s : s + 1, :].astype(jnp.int32)
        target = jnp.sum(jnp.where(label_row == code, sk[s, 0:LEAF, :], 0.0), axis=0, keepdims=True)
        for g in range(NX):
            span = slice(g * 128, (g + 1) * 128)
            emsg[g, 4 * s + 2 : 4 * s + 3, :] = target[:, span]
            emsg[g, 4 * s + 3 : 4 * s + 4, :] = target[:, span]
    send("ex1")
    erecv[me] = emsg[x]

    shared(3, tstat, ztop)
    zlse[2] = joined(tstat[...], [(d, ztop[d]) for d in range(1, NZ)])

    def query_row(which, s):
        return jnp.concatenate([zlse[which, ORDER[4 * s + o4] : ORDER[4 * s + o4] + 1, :] for o4 in range(4)], axis=1)

    weights = xw[...].reshape(256, D)
    class_row = iota((256, SLOTS), 0)
    grad = jnp.zeros((256, D), F32)
    top_losses = []
    for s in range(2):
        scores = ts[s]
        totals = query_row(2, s)
        target = jnp.concatenate([tabs[4 * s + o4, 5:6, :] for o4 in range(4)], axis=1).astype(jnp.int32)
        here = ((target >> 6) & 7) == z
        place = jnp.where(here, ((target >> 9) << 6) + (target & 63), -1)
        hit = class_row == place
        delta = (jnp.exp(scores - totals) - jnp.where(hit, 1.0, 0.0)).astype(BF16)
        score = jnp.sum(jnp.where(hit, scores, 0.0), axis=0, keepdims=True)
        top_losses.append(jnp.where(here, totals - score, 0.0))
        grad = grad + dot(delta, gq[4 * s : 4 * s + 4].reshape(SLOTS, D), NN)
        part[s] = dot(delta, weights, TN)
    tgs[...] = grad.reshape(PLANE, 8, D)

    arrived("ex1")
    pairs = regroup(erecv)
    number = iota((8, SLOTS), 0)
    loss_rows = []
    for s in range(2):
        mine = slotinfo[s : s + 1, :] == number
        leafs = jnp.where(mine, pairs[4 * s : 4 * s + 1, :], 0.0)
        mids = jnp.where(mine, pairs[4 * s + 1 : 4 * s + 2, :], 0.0)
        goal = jnp.where(slotinfo[s : s + 1, :] == 0, pairs[4 * s + 2 : 4 * s + 3, :], 0.0)
        high, mid, low = split3(goal)
        goal = jnp.where(number == 0, high.astype(F32), jnp.where(number == 1, mid.astype(F32), jnp.where(number == 2, low.astype(F32), 0.0)))
        pieces = [piece.astype(F32) for piece in split3(leafs) + split3(mids)]
        pieces = pieces + [jnp.where(mine, 1.0, 0.0), goal]
        rows = dot(jnp.concatenate(pieces, axis=0).astype(BF16), oht[s], NT)
        there = rows[48:56] > 0.5
        leafs = jnp.where(there, rows[0:8] + rows[8:16] + rows[16:24], NEG)
        mids = jnp.where(there, rows[24:32] + rows[32:40] + rows[40:48], NEG)
        loss_rows.append((rows[48:49] > 0.5, rows[56:57] + rows[57:58] + rows[58:59], mids[0:1]))
        for which, values in enumerate((leafs, mids)):
            largest = jnp.max(values, axis=0, keepdims=True)
            total = largest + jnp.log(jnp.sum(jnp.exp(values - largest), axis=0, keepdims=True))
            for o4 in range(4):
                o = ORDER[4 * s + o4]
                stat[which, o : o + 1, :] = total[:, o4 * 128 : (o4 + 1) * 128]

    share(0, stat, zstat)
    send("tg")
    tgr[me] = tgs[me]
    shared(0, stat, zstat)
    for which in range(2):
        zlse[which] = joined(stat[which], [(d, zstat[d, which]) for d in range(1, NZ)])

    for s in range(2):
        pieces = split3(query_row(0, s)) + split3(query_row(1, s))
        pieces = [piece.astype(F32) for piece in pieces] + [jnp.zeros((10, SLOTS), F32)]
        rows = dot(jnp.concatenate(pieces, axis=0).astype(BF16), oht[s], NN)
        leaf_slot = rows[0:1] + rows[1:2] + rows[2:3]
        mid_slot = rows[3:4] + rows[4:5] + rows[5:6]
        for g in range(NX):
            span = slice(g * 128, (g + 1) * 128)
            fmsg[g, 4 * s : 4 * s + 1, :] = leaf_slot[:, span]
            fmsg[g, 4 * s + 1 : 4 * s + 2, :] = mid_slot[:, span]
            fmsg[g, 4 * s + 2 : 4 * s + 3, :] = mid_slot[:, span]
            fmsg[g, 4 * s + 3 : 4 * s + 4, :] = mid_slot[:, span]
    send("ex2")
    frecv[me] = fmsg[x]

    for s in range(2):
        first, goal, middle = loss_rows[s]
        leaf_query = jnp.where(first, query_row(0, s) - goal, 0.0)
        mid_query = jnp.where(first, query_row(1, s) - middle, 0.0)
        for o4 in range(4):
            o = ORDER[4 * s + o4]
            span = slice(o4 * 128, (o4 + 1) * 128)
            losss[o] = jnp.concatenate(
                [top_losses[s][:, span], mid_query[:, span], leaf_query[:, span], jnp.zeros((5, 128), F32)],
                axis=0,
            )

    def losscopy(o):
        return pltpu.make_async_remote_copy(
            src_ref=losss.at[o], dst_ref=lossr.at[o], send_sem=zsend.at[1, o],
            recv_sem=zrecv.at[1, o], device_id=z_id(o), device_id_type=MESH,
        )

    for o in range(1, NZ):
        losscopy(o).start()
        pending.append(losscopy(o).wait_send)

    arrived("ex2")
    scalars = regroup(frecv)
    deltas = []
    for s in (1, 0):
        code = codes[s : s + 1, :].astype(jnp.int32)
        live = code > -2
        hit = jnp.where(label_row == code, 1.0, 0.0)
        delta = jnp.where(live, jnp.exp(sk[s, 0:LEAF, :] - scalars[4 * s : 4 * s + 1, :]) - hit, 0.0)
        middle = jnp.exp(sk[s, LEAF : LEAF + 1, :] - scalars[4 * s + 1 : 4 * s + 2, :])
        middle = jnp.where(live, middle - jnp.where(code >= 0, 1.0, 0.0), 0.0)
        even = odd == 0
        full = jnp.concatenate(
            [
                jnp.where(even, delta, 0.0), jnp.where(even, 0.0, delta),
                jnp.where(even, middle, 0.0), jnp.where(even, 0.0, middle),
                jnp.zeros((14, SLOTS), F32),
            ],
            axis=0,
        ).astype(BF16)
        deltas.append(full)
        ob[s] = dot(full, wext[...], TN).astype(BF16).reshape(PLANE, ROWS, D)
        if s:
            send("ret1")
        pbk[s, me] = ob[s, me]
    arrived("tg")
    tg_sum = tgr[0]
    for f in range(1, PLANE):
        tg_sum = tg_sum + tgr[f]
    tg_ref[pl.ds(pl.multiple_of(dp * 8, 8), 8), :] = tg_sum

    def tgcopy(d, who):
        rows = pl.ds(pl.multiple_of(who * 8, 8), 8)
        return pltpu.make_async_remote_copy(
            src_ref=tg_ref.at[rows], dst_ref=tg_ref.at[rows], send_sem=osend.at[d],
            recv_sem=orecv.at[d], device_id=dp_id(d), device_id_type=MESH,
        )

    for d in range(1, NDP):
        tgcopy(d, dp).start()
        pending.append(tgcopy(d, dp).wait_send)

    halves = (pl.ds(0, 64), pl.ds(64, 64))

    def rs(direction, hop, chunk):
        return pltpu.make_async_remote_copy(
            src_ref=rsS.at[direction, hop, halves[chunk]],
            dst_ref=rsR.at[direction, hop, halves[chunk]],
            send_sem=rssend.at[direction, hop, chunk], recv_sem=rsrecv.at[direction, hop, chunk],
            device_id=z_id(1 if direction == 0 else NZ - 1), device_id_type=MESH,
        )

    def rs_step(direction, hop, chunk):
        o = 4 - hop if direction == 0 else 4 + hop
        index = IDX[o]
        rows = pl.ds((index % 4) * QD + chunk * 64, 64)
        value = part[index // 4, rows, :]
        if hop > 1 or (hop == 1 and chunk == direction):
            rs(direction, hop - 1, chunk).wait_recv()
            value = value + rsR[direction, hop - 1, halves[chunk], :].astype(F32)
        rsS[direction, hop, halves[chunk], :] = value.astype(BF16)
        rs(direction, hop, chunk).start()
        pending.append(rs(direction, hop, chunk).wait_send)

    arrived("ret1")
    send("ret0")
    part[1] = part[1] + dot(oht[1], pbk[1].reshape(SLOTS, D), NN)
    rs_step(0, 0, 0)
    rs_step(1, 0, 1)
    rs_step(0, 1, 1)
    rs_step(1, 1, 0)
    grads = dot(deltas[0], rb[1].reshape(SLOTS, D), NN) + dot(deltas[1], rb[0].reshape(SLOTS, D), NN)
    lg_ref[...] = grads[0:256].reshape(2, LEAF, D)
    mg_ref[...] = grads[256:258]

    def store(n, source, target):
        copy = pltpu.make_async_copy(source, target, outsem.at[n])
        copy.start()
        pending.append(copy.wait)

    store(0, lg_ref, lg_out)
    store(1, mg_ref, mg_out)

    rs_step(0, 1, 0)
    rs_step(1, 1, 1)
    rs_step(1, 2, 0)
    rs_step(1, 2, 1)
    arrived("ret0")
    part[0] = part[0] + dot(oht[0], pbk[0].reshape(SLOTS, D), NN)
    rs_step(0, 2, 1)
    rs_step(0, 2, 0)

    for d in range(1, NDP):
        tgcopy(d, lax.rem(dp - d + NDP, NDP)).wait_recv()
    store(2, tg_ref, tg_out)
    for o in range(1, NZ):
        losscopy(o).wait_recv()
    losses = losss[0]
    for o in range(1, NZ):
        losses = losses + lossr[o]
    loss_ref[...] = losses[0:3]
    store(3, loss_ref, loss_out)

    for direction in range(2):
        for chunk in range(2):
            rs_step(direction, 3, chunk)
    for direction in range(2):
        for chunk in range(2):
            rs(direction, 3, chunk).wait_recv()
    qg_ref[...] = part[0, 0:QD, :] + rsR[0, 3].astype(F32) + rsR[1, 3].astype(F32)
    store(4, qg_ref, qg_out)
    finish()


def place_outputs(*refs):
    for source, target in zip(refs[0:5], refs[5:10]):
        target[...] = source[...]


def per_device(queries, shortlist, slab_slot, top_target, leaf_target, top_weight, mid_weight, leaf_weight):
    hbm = pl.BlockSpec(memory_space=pltpu.HBM)
    vmem = pl.BlockSpec(memory_space=pltpu.VMEM)
    sem = pltpu.SemaphoreType.DMA
    results = (
        jax.ShapeDtypeStruct((QD, D), F32),
        jax.ShapeDtypeStruct((64, D), F32),
        jax.ShapeDtypeStruct((2, D), F32),
        jax.ShapeDtypeStruct((2, LEAF, D), F32),
        jax.ShapeDtypeStruct((3, QD), F32),
    )
    scratch = [
        pltpu.VMEM((NZ, QD, D), BF16),
        pltpu.VMEM((SHORT, QD), jnp.int32),
        pltpu.VMEM((1, BLOCKS), jnp.int32),
        pltpu.VMEM((1, QD), jnp.int32),
        pltpu.VMEM((1, QD), jnp.int32),
        pltpu.VMEM((2, D), BF16),
        pltpu.VMEM((NZ, 8, 128), F32),
        pltpu.VMEM((NZ, 8, 128), F32),
        pltpu.VMEM((NX, 64, D), BF16),
        pltpu.VMEM((272, D), BF16),
        pltpu.VMEM((2, SLOTS, SLOTS), BF16),
        pltpu.VMEM((8, SLOTS), jnp.int32),
        pltpu.VMEM((2, PLANE, ROWS, D), BF16),
        pltpu.VMEM((2, PLANE, ROWS, D), BF16),
        pltpu.VMEM((2, LEAF + 8, SLOTS), F32),
        pltpu.VMEM((2, 256, SLOTS), F32),
        pltpu.VMEM((NX, 8, 128), F32),
        pltpu.VMEM((PLANE, 8, 128), F32),
        pltpu.VMEM((NX, 8, 128), F32),
        pltpu.VMEM((PLANE, 8, 128), F32),
        pltpu.VMEM((NX, 8, 128), F32),
        pltpu.VMEM((PLANE, 8, 128), F32),
        pltpu.VMEM((2, NZ, 128), F32),
        pltpu.VMEM((NZ, 2, NZ, 128), F32),
        pltpu.VMEM((3, NZ, 128), F32),
        pltpu.VMEM((NZ, 128), F32),
        pltpu.VMEM((NZ, NZ, 128), F32),
        pltpu.VMEM((2, SLOTS, D), F32),
        pltpu.VMEM((2, PLANE, ROWS, D), BF16),
        pltpu.VMEM((2, PLANE, ROWS, D), BF16),
        pltpu.VMEM((PLANE, 8, D), F32),
        pltpu.VMEM((PLANE, 8, D), F32),
        pltpu.VMEM((NZ, 8, 128), F32),
        pltpu.VMEM((NZ, 8, 128), F32),
        pltpu.VMEM((2, 4, QD, D), BF16),
        pltpu.VMEM((2, 4, QD, D), BF16),
        *[pltpu.VMEM(result.shape, F32) for result in results],
        sem((8,)), sem((8,)),
        sem((2, 4, 2)), sem((2, 4, 2)),
        sem((2, 4, 2)), sem((2, 4, 2)),
        sem((4, NZ)), sem((4, NZ)),
        sem((NX,)), sem((NX,)),
        sem((NDP,)), sem((NDP,)),
        sem((9,)), sem((5,)),
    ]
    arrays = pl.pallas_call(
        kernel,
        out_shape=results,
        in_specs=[hbm] * 8,
        out_specs=(hbm,) * 5,
        scratch_shapes=scratch,
        compiler_params=pltpu.CompilerParams(
            collective_id=0, has_side_effects=True, vmem_limit_bytes=60 << 20
        ),
    )(
        queries, shortlist.T, slab_slot.reshape(1, -1), top_target.reshape(1, -1), leaf_target.reshape(1, -1),
        leaf_weight, mid_weight, top_weight,
    )
    return pl.pallas_call(
        place_outputs,
        out_shape=results,
        in_specs=[vmem] * 5,
        out_specs=(vmem,) * 5,
        compiler_params=pltpu.CompilerParams(vmem_limit_bytes=60 << 20),
    )(*arrays)


def solution(mesh):
    both = ("dp", "label")
    in_specs = (
        P(both, None), P(both, None), P(), P(both), P(both),
        P("label", None), P(both, None), P(both, None, None),
    )
    out_specs = (
        P(both, None), P("label", None), P(both, None), P(both, None, None), P(None, both),
    )
    return jax.shard_map(
        per_device, mesh=mesh, in_specs=in_specs, out_specs=out_specs, check_vma=False
    )
```

time: 102 us -> 85.7 us (0.84)
  the two profiles are of different devices: /device:TPU:1 before, /device:TPU:8 now
where the time goes in v1:
time: 85.7 us; the launch traced here: 84.6 us
  Pallas kernels  84 us (98%)
    pallas_call x1, Pallas kernels, per_device(): pl.pallas_call(kernel, out_shape=results, in_specs=[hbm] * 8, out_specs=(...  81.8 us
    pallas_call x1, Pallas kernels, per_device(): pl.pallas_call(place_outputs, out_shape=results, in_specs=[vmem] * 5, out...  2.12 us

profile of v1, /device:TPU:8, one launch (start us, length us, event | category | flops | bytes accessed | tf_op | source)
XLA Modules:
  0.0 84.6 jit_solution(16676879572876553140)
XLA Ops:
  0.6 81.8 %shard_map.119 = (f32[128,512]{1,0:T(8,128)}, f32[64,512]{1,0:T(8,128)}, f32[2,512]{1,0:T(2,128)}, f32[2,128,512]{2,1,0:T(8,128)}, f32[3,128]{1,0:T(4,128)}) custom-call(bf16[128,512]{1,0:T(8,128)(2,1)} %query_in.1, s32[4,128]{1,0:T(4,128)} %bitcast.4, s32[1,512]{1,0:T(1,128)} %bitcast.5, s32[1,128]{1,0:T(1,128)} %bitcast.6, s32[1,128]{1,0:T(1,128)} %bitcast.7, ...), custom_call_target="tpu_custom_call" | custom-call | tf_op jit(solution)/shard_map/pallas_call | solution.py:627
  82.5 2.1 %shard_map.120 = (f32[128,512]{1,0:T(8,128)}, f32[64,512]{1,0:T(8,128)}, f32[2,512]{1,0:T(2,128)}, f32[2,128,512]{2,1,0:T(8,128)}, f32[3,128]{1,0:T(4,128)}) custom-call(f32[128,512]{1,0:T(8,128)} %get-tuple-element.10.refs_0_, f32[64,512]{1,0:T(8,128)} %get-tuple-element.11.refs_1_, f32[2,512]{1,0:T(2,128)} %get-tuple-element.12.refs_2_, ...), custom_call_target="tpu_custom_call" | custom-call | tf_op jit(solution)/shard_map/pallas_call | solution.py:640

commit v2 on v1

--- a/solution.py
+++ b/solution.py
@@ -14,8 +14,10 @@
 NX = 4
 NDP = 8
 PLANE = NX * NDP
-ROWS = 16
+STEPS = 4
+ROWS = 8
 SLOTS = PLANE * ROWS
+GROUPS = 2
 ORDER = (0, 1, 7, 2, 6, 3, 5, 4)
 IDX = tuple(ORDER.index(o) for o in range(NZ))
 NEG = -1e30
@@ -47,8 +49,8 @@
     query_in, short_in, slab_in, target_in, leaftarget_in, leaf_in, mid_in, topw_in,
     qg_out, tg_out, mg_out, lg_out, loss_out,
     gq, short_ref, slab_ref, target_ref, leaftarget_ref, mid_ref, tab, tabs,
-    xw, wext, oht, slotinfo, pk, rb, sk, ts, cmsg, crecv, emsg, erecv, fmsg, frecv,
-    stat, zstat, zlse, tstat, ztop, part, ob, pbk, tgs, tgr, losss, lossr, rsS, rsR,
+    xw, wext, oht, slotinfo, pk, rb, sk, ts, cmsg, crecv, emsg, erecv, gmsg, grecv, fmsg, frecv,
+    stat, zstat, zlse, tstat, ztop, part, ob, pbk, tgs, tgx, tgt, tgr, losss, lossr, rsS, rsR,
     qg_ref, tg_ref, mg_ref, lg_ref, loss_ref,
     psend, precv, agsend, agrecv, rssend, rsrecv, zsend, zrecv, wsend, wrecv, osend, orecv, insem, outsem,
 ):
@@ -146,15 +148,14 @@
 
     span31 = pl.ds(0, PLANE - 1)
     exchanges = {
-        "rows0": (0, lambda tx, td: pk.at[0, tx * NDP + td], rb.at[0]),
-        "rows1": (1, lambda tx, td: pk.at[1, tx * NDP + td], rb.at[1]),
-        "code": (2, lambda tx, td: cmsg.at[tx], crecv),
-        "ex1": (3, lambda tx, td: emsg.at[tx], erecv),
-        "ex2": (4, lambda tx, td: fmsg.at[tx], frecv),
-        "ret1": (5, lambda tx, td: ob.at[1, tx * NDP + td], pbk.at[1]),
-        "ret0": (6, lambda tx, td: ob.at[0, tx * NDP + td], pbk.at[0]),
-        "tg": (7, lambda tx, td: tgs.at[tx * NDP + td], tgr),
+        "code": (8, lambda tx, td: cmsg.at[tx // 2], crecv),
+        "ex1": (9, lambda tx, td: emsg.at[tx // 2], erecv),
+        "goal": (10, lambda tx, td: gmsg.at[tx // 2], grecv),
+        "ex2": (11, lambda tx, td: fmsg.at[tx // 2], frecv),
     }
+    for t in range(STEPS):
+        exchanges[f"rows{t}"] = (t, lambda tx, td, t=t: pk.at[t, tx * NDP + td], rb.at[t])
+        exchanges[f"ret{t}"] = (4 + t, lambda tx, td, t=t: ob.at[t, tx * NDP + td], pbk.at[t])
 
     def whole(name):
         phase, _, target = exchanges[name]
@@ -172,24 +173,29 @@
     lane = iota((8, 128), 1)
 
     def regroup(received):
+        mine = lax.rem(x, 2) * NDP + dp
         groups = []
-        for g in range(NX):
+        for g in range(GROUPS):
             out = jnp.zeros((8, 128), F32)
-            for j in range(NDP):
-                turned = pltpu.roll(received[g * NDP + j], lax.rem(j - dp + NDP, NDP) * ROWS, axis=1)
+            for j in range(16):
+                turned = pltpu.roll(received[g * 16 + j], lax.rem(j - mine + 16, 16) * ROWS, axis=1)
                 out = jnp.where(lane // ROWS == j, turned, out)
             groups.append(out)
         return jnp.concatenate(groups, axis=1)
 
+    def spread(message, row, value):
+        for g in range(GROUPS):
+            message[g, row : row + 1, :] = value[:, g * 128 : (g + 1) * 128]
+
     for load in loads[1:5]:
         load.wait()
-    wide = iota((QD, SLOTS), 1)
+    wide = iota((QD, BLOCKS), 1)
     narrow = iota((QD, QD), 1)
     query_col = iota((QD, 1), 0)
     eye = iota((QD, QD), 0) == narrow
     slab = slab_ref[...].astype(F32)
     lower = jnp.where(iota((QD, QD), 1) < iota((QD, QD), 0), 1.0, 0.0).astype(BF16)
-    base = jnp.zeros((1, SLOTS), F32)
+    base = jnp.zeros((1, BLOCKS), F32)
     table = jnp.zeros((QD, QD), F32)
     for j in range(SHORT):
         named = jnp.sum(jnp.where(eye, short_ref[j : j + 1, :].astype(F32), 0.0), axis=1, keepdims=True).astype(jnp.int32)
@@ -205,8 +211,9 @@
         index = jnp.zeros((QD, 1), jnp.int32)
         for o in range(NZ):
             index = jnp.where(offset == o, IDX[o], index)
-        place = holder_dp * ROWS + (position & 1) * 8 + (index & 3) * 2 + rank
-        row = holder_z * NX + holder_x
+        holder = holder_x * NDP + holder_dp
+        place = (holder & 15) * ROWS + (position & 1) * 4 + (index & 1) * 2 + rank
+        row = holder_z * 4 + ((index >> 1) & 1) * GROUPS + (holder >> 4)
         left = jnp.where(narrow == row, (query_col + 1).astype(F32), jnp.where(narrow == row + 32, j * 128.0, 0.0))
         right = jnp.where(narrow == place, 1.0, 0.0)
         table = table + dot(left.astype(BF16), right.astype(BF16), TN)
@@ -230,70 +237,78 @@
 
     qid = iota((SLOTS, SLOTS), 0)
 
-    def pack(s):
-        ids = jnp.zeros((4, 128), jnp.int32)
-        order = jnp.zeros((4, 128), jnp.int32)
+    def queries_of(t):
+        return gq[2 * t : 2 * t + 2].reshape(SLOTS, D)
+
+    def pack(t):
+        ids = jnp.zeros((GROUPS, 128), jnp.int32)
+        order = jnp.zeros((GROUPS, 128), jnp.int32)
         targets = []
-        for o4 in range(4):
-            tile = tabs[4 * s + o4].astype(jnp.int32)
-            value = tile[0:4]
-            ids = ids + jnp.where(value > 0, ((value - 1) & 127) + o4 * QD + 1, 0)
+        half = GROUPS * (t % 2)
+        for o2 in range(2):
+            tile = tabs[2 * t + o2].astype(jnp.int32)
+            value = tile[half : half + GROUPS]
+            ids = ids + jnp.where(value > 0, ((value - 1) & 127) + o2 * QD + 1, 0)
             order = order + jnp.where(value > 0, (value - 1) >> 7, 0)
             targets.append(tile[4:5].astype(F32))
-        ids = jnp.concatenate([ids[g : g + 1] for g in range(NX)], axis=1)
-        order = jnp.concatenate([order[g : g + 1] for g in range(NX)], axis=1)
+        ids = jnp.concatenate([ids[g : g + 1] for g in range(GROUPS)], axis=1)
+        order = jnp.concatenate([order[g : g + 1] for g in range(GROUPS)], axis=1)
         live = ids > 0
         hot = jnp.where(qid == ids - 1, 1.0, 0.0).astype(BF16)
-        oht[s] = hot
-        queries = gq[4 * s : 4 * s + 4].reshape(SLOTS, D)
-        pk[s] = dot(hot, queries, TN).astype(BF16).reshape(PLANE, ROWS, D)
-        slotinfo[s : s + 1, :] = jnp.where(live, order, -1)
+        oht[t] = hot
+        pk[t] = dot(hot, queries_of(t), TN).astype(BF16).reshape(PLANE, ROWS, D)
+        send(f"rows{t}")
+        rb[t, me] = pk[t, me]
+        slotinfo[t : t + 1, :] = jnp.where(live, order, -1)
         wanted = jnp.broadcast_to(jnp.concatenate(targets, axis=1), (8, SLOTS)).astype(BF16)
         code = dot(wanted, hot, NN)[0:1, :]
-        code = jnp.where(live, jnp.where(order == 0, code, -1.0), -2.0)
-        for g in range(NX):
-            cmsg[g, s : s + 1, :] = code[:, g * 128 : (g + 1) * 128]
-
-    def top_scores(s):
-        queries = gq[4 * s : 4 * s + 4].reshape(SLOTS, D)
-        scores = dot(xw[...].reshape(256, D), queries, NT)
-        ts[s] = scores
+        spread(cmsg, t, jnp.where(live, jnp.where(order == 0, code, -1.0), -2.0))
+
+    def top_scores(t):
+        scores = dot(xw[...].reshape(256, D), queries_of(t), NT)
+        ts[t] = scores
         largest = jnp.max(scores, axis=0, keepdims=True)
         total = largest + jnp.log(jnp.sum(jnp.exp(scores - largest), axis=0, keepdims=True))
-        for o4 in range(4):
-            o = ORDER[4 * s + o4]
-            tstat[o : o + 1, :] = total[:, o4 * 128 : (o4 + 1) * 128]
-
-    for hop in (2, 3):
-        for direction, chunk in flows(hop):
-            ag(direction, hop - 1, chunk).wait_recv()
-            ag_start(direction, hop, chunk)
+        for o2 in range(2):
+            o = ORDER[2 * t + o2]
+            tstat[o : o + 1, :] = total[:, o2 * 128 : (o2 + 1) * 128]
+
+    def forward(hop, direction):
+        for chunk in range(2):
+            if hop < 4 or chunk == direction:
+                ag(direction, hop - 1, chunk).wait_recv()
+                ag_start(direction, hop, chunk)
+
+    for direction in range(2):
+        forward(2, direction)
     for d in range(1, NZ):
         tabcopy(d).wait_recv()
     pack(0)
-    send("rows0")
-    rb[0, me] = pk[0, me]
-    for direction, chunk in flows(4):
-        ag(direction, 3, chunk).wait_recv()
-        ag_start(direction, 4, chunk)
+    for direction in range(2):
+        forward(3, direction)
+    pack(1)
     for d in range(1, NX):
         wcopy(d, lax.rem(x - d + NX, NX)).wait_recv()
+    top_scores(0)
+    for direction in range(2):
+        forward(4, direction)
+    ag(1, 3, 0).wait_recv()
+    pack(2)
     for load in loads[6:9]:
         load.wait()
     wext[256:272, :] = jnp.concatenate([mid_ref[...].astype(F32), jnp.zeros((14, D), F32)], axis=0).astype(BF16)
-    for g in range(NX):
-        cmsg[g, 2:8, :] = jnp.zeros((6, 128), F32)
-    top_scores(0)
-    for direction, chunk in ((1, 0), (0, 1)):
-        ag(direction, 3, chunk).wait_recv()
+    for g in range(GROUPS):
+        cmsg[g, 4:8, :] = jnp.zeros((4, 128), F32)
+        gmsg[g, 4:8, :] = jnp.zeros((4, 128), F32)
+    top_scores(1)
+    ag(0, 3, 1).wait_recv()
     for direction, chunk in flows(4):
         ag(direction, 4, chunk).wait_recv()
-    pack(1)
-    send("rows1")
+    pack(3)
     send("code")
-    rb[1, me] = pk[1, me]
-    crecv[me] = cmsg[x]
-    top_scores(1)
+    crecv[me] = cmsg[x // 2]
+    top_scores(2)
+    top_scores(3)
 
     def zshare(slot, source, target, d):
         return pltpu.make_async_remote_copy(
@@ -322,7 +337,7 @@
 
     share(3, tstat, ztop)
 
-    odd = (iota((1, SLOTS), 1) >> 3) & 1
+    odd = (iota((1, SLOTS), 1) >> 2) & 1
 
     def holder_scores(s):
         scores = dot(wext[...], rb[s].reshape(SLOTS, D), NT)
@@ -333,111 +348,110 @@
         chosen = sk[s, 0:LEAF, :]
         largest = jnp.max(chosen, axis=0, keepdims=True)
         total = largest + jnp.log(jnp.sum(jnp.exp(chosen - largest), axis=0, keepdims=True))
-        middle = sk[s, LEAF : LEAF + 1, :]
-        for g in range(NX):
-            span = slice(g * 128, (g + 1) * 128)
-            emsg[g, 4 * s : 4 * s + 1, :] = total[:, span]
-            emsg[g, 4 * s + 1 : 4 * s + 2, :] = middle[:, span]
-
-    arrived("rows0")
-    holder_scores(0)
-    arrived("rows1")
-    holder_scores(1)
+        spread(emsg, 2 * s, total)
+        spread(emsg, 2 * s + 1, sk[s, LEAF : LEAF + 1, :])
+
+    for t in range(STEPS):
+        arrived(f"rows{t}")
+        holder_scores(t)
+    send("ex1")
+    erecv[me] = emsg[x // 2]
     arrived("code")
     codes = regroup(crecv)
     label_row = iota((LEAF, SLOTS), 0)
-    for s in range(2):
-        code = codes[s : s + 1, :].astype(jnp.int32)
-        target = jnp.sum(jnp.where(label_row == code, sk[s, 0:LEAF, :], 0.0), axis=0, keepdims=True)
-        for g in range(NX):
-            span = slice(g * 128, (g + 1) * 128)
-            emsg[g, 4 * s + 2 : 4 * s + 3, :] = target[:, span]
-            emsg[g, 4 * s + 3 : 4 * s + 4, :] = target[:, span]
-    send("ex1")
-    erecv[me] = emsg[x]
+    for t in range(STEPS):
+        code = codes[t : t + 1, :].astype(jnp.int32)
+        spread(gmsg, t, jnp.sum(jnp.where(label_row == code, sk[t, 0:LEAF, :], 0.0), axis=0, keepdims=True))
 
     shared(3, tstat, ztop)
     zlse[2] = joined(tstat[...], [(d, ztop[d]) for d in range(1, NZ)])
 
-    def query_row(which, s):
-        return jnp.concatenate([zlse[which, ORDER[4 * s + o4] : ORDER[4 * s + o4] + 1, :] for o4 in range(4)], axis=1)
+    def query_row(which, t):
+        return jnp.concatenate([zlse[which, ORDER[2 * t + o2] : ORDER[2 * t + o2] + 1, :] for o2 in range(2)], axis=1)
 
     weights = xw[...].reshape(256, D)
     class_row = iota((256, SLOTS), 0)
     grad = jnp.zeros((256, D), F32)
     top_losses = []
-    for s in range(2):
-        scores = ts[s]
-        totals = query_row(2, s)
-        target = jnp.concatenate([tabs[4 * s + o4, 5:6, :] for o4 in range(4)], axis=1).astype(jnp.int32)
+    for t in range(STEPS):
+        scores = ts[t]
+        totals = query_row(2, t)
+        target = jnp.concatenate([tabs[2 * t + o2, 5:6, :] for o2 in range(2)], axis=1).astype(jnp.int32)
         here = ((target >> 6) & 7) == z
         place = jnp.where(here, ((target >> 9) << 6) + (target & 63), -1)
         hit = class_row == place
         delta = (jnp.exp(scores - totals) - jnp.where(hit, 1.0, 0.0)).astype(BF16)
         score = jnp.sum(jnp.where(hit, scores, 0.0), axis=0, keepdims=True)
         top_losses.append(jnp.where(here, totals - score, 0.0))
-        grad = grad + dot(delta, gq[4 * s : 4 * s + 4].reshape(SLOTS, D), NN)
-        part[s] = dot(delta, weights, TN)
-    tgs[...] = grad.reshape(PLANE, 8, D)
+        grad = grad + dot(delta, queries_of(t), NN)
+        part[t] = dot(delta, weights, TN)
+    core = lax.rem(dp, 2)
+    for p in range(PLANE):
+        tgs[p % 2, p // 2] = grad[8 * p : 8 * p + 8]
+    pair_copy = pltpu.make_async_remote_copy(
+        src_ref=tgs.at[1 - core], dst_ref=tgx, send_sem=osend.at[0], recv_sem=orecv.at[0],
+        device_id=(dp + 1 - 2 * core, label), device_id_type=MESH,
+    )
+    pair_copy.start()
+    pending.append(pair_copy.wait_send)
+
+    def tg_partner(i):
+        return lax.rem(x + i // 4, NX), lax.rem(dp // 2 + i % 4, 4)
+
+    def tg_remote(source, target, i):
+        tx, ty = tg_partner(i)
+        return pltpu.make_async_remote_copy(
+            src_ref=source, dst_ref=target, send_sem=psend.at[12], recv_sem=precv.at[12],
+            device_id=(ty * 2 + core, tx * NZ + z), device_id_type=MESH,
+        )
+
+    tg_whole = tg_remote(tgr.at[pl.ds(0, 15)], tgr.at[pl.ds(0, 15)], 1)
 
     arrived("ex1")
     pairs = regroup(erecv)
     number = iota((8, SLOTS), 0)
     loss_rows = []
-    for s in range(2):
-        mine = slotinfo[s : s + 1, :] == number
-        leafs = jnp.where(mine, pairs[4 * s : 4 * s + 1, :], 0.0)
-        mids = jnp.where(mine, pairs[4 * s + 1 : 4 * s + 2, :], 0.0)
-        goal = jnp.where(slotinfo[s : s + 1, :] == 0, pairs[4 * s + 2 : 4 * s + 3, :], 0.0)
-        high, mid, low = split3(goal)
-        goal = jnp.where(number == 0, high.astype(F32), jnp.where(number == 1, mid.astype(F32), jnp.where(number == 2, low.astype(F32), 0.0)))
+    for t in range(STEPS):
+        mine = slotinfo[t : t + 1, :] == number
+        leafs = jnp.where(mine, pairs[2 * t : 2 * t + 1, :], 0.0)
+        mids = jnp.where(mine, pairs[2 * t + 1 : 2 * t + 2, :], 0.0)
         pieces = [piece.astype(F32) for piece in split3(leafs) + split3(mids)]
-        pieces = pieces + [jnp.where(mine, 1.0, 0.0), goal]
-        rows = dot(jnp.concatenate(pieces, axis=0).astype(BF16), oht[s], NT)
+        pieces = pieces + [jnp.where(mine, 1.0, 0.0), jnp.zeros((8, SLOTS), F32)]
+        rows = dot(jnp.concatenate(pieces, axis=0).astype(BF16), oht[t], NT)
         there = rows[48:56] > 0.5
         leafs = jnp.where(there, rows[0:8] + rows[8:16] + rows[16:24], NEG)
         mids = jnp.where(there, rows[24:32] + rows[32:40] + rows[40:48], NEG)
-        loss_rows.append((rows[48:49] > 0.5, rows[56:57] + rows[57:58] + rows[58:59], mids[0:1]))
+        loss_rows.append((there[0:1], mids[0:1]))
         for which, values in enumerate((leafs, mids)):
             largest = jnp.max(values, axis=0, keepdims=True)
             total = largest + jnp.log(jnp.sum(jnp.exp(values - largest), axis=0, keepdims=True))
-            for o4 in range(4):
-                o = ORDER[4 * s + o4]
-                stat[which, o : o + 1, :] = total[:, o4 * 128 : (o4 + 1) * 128]
+            for o2 in range(2):
+                o = ORDER[2 * t + o2]
+                stat[which, o : o + 1, :] = total[:, o2 * 128 : (o2 + 1) * 128]
 
     share(0, stat, zstat)
-    send("tg")
-    tgr[me] = tgs[me]
+    pair_copy.wait_recv()
+    own = x * 4 + dp // 2
+    tgt[...] = tgs[core] + tgx[...]
+    for i in range(1, 16):
+        tx, ty = tg_partner(i)
+        tg_remote(tgt.at[tx * 4 + ty], tgr.at[own], i).start()
+    pending.append(tg_whole.wait_send)
+    tgr[own] = tgt[own]
     shared(0, stat, zstat)
     for which in range(2):
         zlse[which] = joined(stat[which], [(d, zstat[d, which]) for d in range(1, NZ)])
 
-    for s in range(2):
-        pieces = split3(query_row(0, s)) + split3(query_row(1, s))
+    for t in range(STEPS):
+        pieces = split3(query_row(0, t)) + split3(query_row(1, t))
         pieces = [piece.astype(F32) for piece in pieces] + [jnp.zeros((10, SLOTS), F32)]
-        rows = dot(jnp.concatenate(pieces, axis=0).astype(BF16), oht[s], NN)
-        leaf_slot = rows[0:1] + rows[1:2] + rows[2:3]
-        mid_slot = rows[3:4] + rows[4:5] + rows[5:6]
-        for g in range(NX):
-            span = slice(g * 128, (g + 1) * 128)
-            fmsg[g, 4 * s : 4 * s + 1, :] = leaf_slot[:, span]
-            fmsg[g, 4 * s + 1 : 4 * s + 2, :] = mid_slot[:, span]
-            fmsg[g, 4 * s + 2 : 4 * s + 3, :] = mid_slot[:, span]
-            fmsg[g, 4 * s + 3 : 4 * s + 4, :] = mid_slot[:, span]
+        rows = dot(jnp.concatenate(pieces, axis=0).astype(BF16), oht[t], NN)
+        spread(fmsg, 2 * t, rows[0:1] + rows[1:2] + rows[2:3])
+        spread(fmsg, 2 * t + 1, rows[3:4] + rows[4:5] + rows[5:6])
     send("ex2")
-    frecv[me] = fmsg[x]
-
-    for s in range(2):
-        first, goal, middle = loss_rows[s]
-        leaf_query = jnp.where(first, query_row(0, s) - goal, 0.0)
-        mid_query = jnp.where(first, query_row(1, s) - middle, 0.0)
-        for o4 in range(4):
-            o = ORDER[4 * s + o4]
-            span = slice(o4 * 128, (o4 + 1) * 128)
-            losss[o] = jnp.concatenate(
-                [top_losses[s][:, span], mid_query[:, span], leaf_query[:, span], jnp.zeros((5, 128), F32)],
-                axis=0,
-            )
+    frecv[me] = fmsg[x // 2]
+    send("goal")
+    grecv[me] = gmsg[x // 2]
 
     def losscopy(o):
         return pltpu.make_async_remote_copy(
@@ -445,21 +459,18 @@
             recv_sem=zrecv.at[1, o], device_id=z_id(o), device_id_type=MESH,
         )
 
-    for o in range(1, NZ):
-        losscopy(o).start()
-        pending.append(losscopy(o).wait_send)
-
     arrived("ex2")
     scalars = regroup(frecv)
-    deltas = []
-    for s in (1, 0):
-        code = codes[s : s + 1, :].astype(jnp.int32)
+    even = odd == 0
+    deltas = [None] * STEPS
+
+    def back_rows(t):
+        code = codes[t : t + 1, :].astype(jnp.int32)
         live = code > -2
         hit = jnp.where(label_row == code, 1.0, 0.0)
-        delta = jnp.where(live, jnp.exp(sk[s, 0:LEAF, :] - scalars[4 * s : 4 * s + 1, :]) - hit, 0.0)
-        middle = jnp.exp(sk[s, LEAF : LEAF + 1, :] - scalars[4 * s + 1 : 4 * s + 2, :])
+        delta = jnp.where(live, jnp.exp(sk[t, 0:LEAF, :] - scalars[2 * t : 2 * t + 1, :]) - hit, 0.0)
+        middle = jnp.exp(sk[t, LEAF : LEAF + 1, :] - scalars[2 * t + 1 : 2 * t + 2, :])
         middle = jnp.where(live, middle - jnp.where(code >= 0, 1.0, 0.0), 0.0)
-        even = odd == 0
         full = jnp.concatenate(
             [
                 jnp.where(even, delta, 0.0), jnp.where(even, 0.0, delta),
@@ -468,14 +479,20 @@
             ],
             axis=0,
         ).astype(BF16)
-        deltas.append(full)
-        ob[s] = dot(full, wext[...], TN).astype(BF16).reshape(PLANE, ROWS, D)
-        if s:
-            send("ret1")
-        pbk[s, me] = ob[s, me]
-    arrived("tg")
+        deltas[t] = full
+        ob[t] = dot(full, wext[...], TN).astype(BF16).reshape(PLANE, ROWS, D)
+
+    def send_back(t):
+        send(f"ret{t}")
+        pbk[t, me] = ob[t, me]
+
+    for t in (3, 2, 1, 0):
+        back_rows(t)
+        send_back(t)
+
+    tg_whole.wait_recv()
     tg_sum = tgr[0]
-    for f in range(1, PLANE):
+    for f in range(1, PLANE // 2):
         tg_sum = tg_sum + tgr[f]
     tg_ref[pl.ds(pl.multiple_of(dp * 8, 8), 8), :] = tg_sum
 
@@ -489,6 +506,33 @@
     for d in range(1, NDP):
         tgcopy(d, dp).start()
         pending.append(tgcopy(d, dp).wait_send)
+
+    def send_losses():
+        arrived("goal")
+        goals = regroup(grecv)
+        for t in range(STEPS):
+            goal = jnp.where(slotinfo[t : t + 1, :] == 0, goals[t : t + 1, :], 0.0)
+            pieces = [piece.astype(F32) for piece in split3(goal)] + [jnp.zeros((13, SLOTS), F32)]
+            rows = dot(jnp.concatenate(pieces, axis=0).astype(BF16), oht[t], NT)
+            first, middle = loss_rows[t]
+            leaf_query = jnp.where(first, query_row(0, t) - (rows[0:1] + rows[1:2] + rows[2:3]), 0.0)
+            mid_query = jnp.where(first, query_row(1, t) - middle, 0.0)
+            for o2 in range(2):
+                o = ORDER[2 * t + o2]
+                span = slice(o2 * 128, (o2 + 1) * 128)
+                losss[o] = jnp.concatenate(
+                    [top_losses[t][:, span], mid_query[:, span], leaf_query[:, span], jnp.zeros((5, 128), F32)],
+                    axis=0,
+                )
+        for o in range(1, NZ):
+            losscopy(o).start()
+            pending.append(losscopy(o).wait_send)
+
+
+    def store(n, source, target):
+        copy = pltpu.make_async_copy(source, target, outsem.at[n])
+        copy.start()
+        pending.append(copy.wait)
 
     halves = (pl.ds(0, 64), pl.ds(64, 64))
 
@@ -503,8 +547,8 @@
     def rs_step(direction, hop, chunk):
         o = 4 - hop if direction == 0 else 4 + hop
         index = IDX[o]
-        rows = pl.ds((index % 4) * QD + chunk * 64, 64)
-        value = part[index // 4, rows, :]
+        rows = pl.ds((index % 2) * QD + chunk * 64, 64)
+        value = part[index // 2, rows, :]
         if hop > 1 or (hop == 1 and chunk == direction):
             rs(direction, hop - 1, chunk).wait_recv()
             value = value + rsR[direction, hop - 1, halves[chunk], :].astype(F32)
@@ -512,33 +556,36 @@
         rs(direction, hop, chunk).start()
         pending.append(rs(direction, hop, chunk).wait_send)
 
-    arrived("ret1")
-    send("ret0")
-    part[1] = part[1] + dot(oht[1], pbk[1].reshape(SLOTS, D), NN)
+    def returned(t):
+        arrived(f"ret{t}")
+        part[t] = part[t] + dot(oht[t], pbk[t].reshape(SLOTS, D), NN)
+
+    returned(3)
     rs_step(0, 0, 0)
     rs_step(1, 0, 1)
+    rs_step(1, 1, 0)
+    returned(2)
     rs_step(0, 1, 1)
-    rs_step(1, 1, 0)
-    grads = dot(deltas[0], rb[1].reshape(SLOTS, D), NN) + dot(deltas[1], rb[0].reshape(SLOTS, D), NN)
+    rs_step(1, 1, 1)
+    rs_step(0, 1, 0)
+    rs_step(1, 2, 0)
+    send_losses()
+    rs_step(1, 2, 1)
+    returned(1)
+    rs_step(0, 2, 1)
+    rs_step(1, 3, 0)
+    rs_step(0, 2, 0)
+    rs_step(1, 3, 1)
+    grads = jnp.zeros((272, D), F32)
+    for t in range(STEPS):
+        grads = grads + dot(deltas[t], rb[t].reshape(SLOTS, D), NN)
     lg_ref[...] = grads[0:256].reshape(2, LEAF, D)
     mg_ref[...] = grads[256:258]
-
-    def store(n, source, target):
-        copy = pltpu.make_async_copy(source, target, outsem.at[n])
-        copy.start()
-        pending.append(copy.wait)
-
     store(0, lg_ref, lg_out)
     store(1, mg_ref, mg_out)
-
-    rs_step(0, 1, 0)
-    rs_step(1, 1, 1)
-    rs_step(1, 2, 0)
-    rs_step(1, 2, 1)
-    arrived("ret0")
-    part[0] = part[0] + dot(oht[0], pbk[0].reshape(SLOTS, D), NN)
-    rs_step(0, 2, 1)
-    rs_step(0, 2, 0)
+    returned(0)
+    rs_step(0, 3, 1)
+    rs_step(0, 3, 0)
 
     for d in range(1, NDP):
         tgcopy(d, lax.rem(dp - d + NDP, NDP)).wait_recv()
@@ -550,13 +597,10 @@
         losses = losses + lossr[o]
     loss_ref[...] = losses[0:3]
     store(3, loss_ref, loss_out)
-
-    for direction in range(2):
-        for chunk in range(2):
-            rs_step(direction, 3, chunk)
-    for direction in range(2):
-        for chunk in range(2):
-            rs(direction, 3, chunk).wait_recv()
+    for chunk in (0, 1):
+        rs(1, 3, chunk).wait_recv()
+    for chunk in (1, 0):
+        rs(0, 3, chunk).wait_recv()
     qg_ref[...] = part[0, 0:QD, :] + rsR[0, 3].astype(F32) + rsR[1, 3].astype(F32)
     store(4, qg_ref, qg_out)
     finish()
@@ -589,34 +633,38 @@
         pltpu.VMEM((NZ, 8, 128), F32),
         pltpu.VMEM((NX, 64, D), BF16),
         pltpu.VMEM((272, D), BF16),
-        pltpu.VMEM((2, SLOTS, SLOTS), BF16),
+        pltpu.VMEM((STEPS, SLOTS, SLOTS), BF16),
         pltpu.VMEM((8, SLOTS), jnp.int32),
-        pltpu.VMEM((2, PLANE, ROWS, D), BF16),
-        pltpu.VMEM((2, PLANE, ROWS, D), BF16),
-        pltpu.VMEM((2, LEAF + 8, SLOTS), F32),
-        pltpu.VMEM((2, 256, SLOTS), F32),
-        pltpu.VMEM((NX, 8, 128), F32),
+        pltpu.VMEM((STEPS, PLANE, ROWS, D), BF16),
+        pltpu.VMEM((STEPS, PLANE, ROWS, D), BF16),
+        pltpu.VMEM((STEPS, LEAF + 8, SLOTS), F32),
+        pltpu.VMEM((STEPS, 256, SLOTS), F32),
+        pltpu.VMEM((GROUPS, 8, 128), F32),
         pltpu.VMEM((PLANE, 8, 128), F32),
-        pltpu.VMEM((NX, 8, 128), F32),
+        pltpu.VMEM((GROUPS, 8, 128), F32),
         pltpu.VMEM((PLANE, 8, 128), F32),
-        pltpu.VMEM((NX, 8, 128), F32),
+        pltpu.VMEM((GROUPS, 8, 128), F32),
+        pltpu.VMEM((PLANE, 8, 128), F32),
+        pltpu.VMEM((GROUPS, 8, 128), F32),
         pltpu.VMEM((PLANE, 8, 128), F32),
         pltpu.VMEM((2, NZ, 128), F32),
         pltpu.VMEM((NZ, 2, NZ, 128), F32),
         pltpu.VMEM((3, NZ, 128), F32),
         pltpu.VMEM((NZ, 128), F32),
         pltpu.VMEM((NZ, NZ, 128), F32),
-        pltpu.VMEM((2, SLOTS, D), F32),
-        pltpu.VMEM((2, PLANE, ROWS, D), BF16),
-        pltpu.VMEM((2, PLANE, ROWS, D), BF16),
-        pltpu.VMEM((PLANE, 8, D), F32),
-        pltpu.VMEM((PLANE, 8, D), F32),
+        pltpu.VMEM((STEPS, SLOTS, D), F32),
+        pltpu.VMEM((STEPS, PLANE, ROWS, D), BF16),
+        pltpu.VMEM((STEPS, PLANE, ROWS, D), BF16),
+        pltpu.VMEM((2, PLANE // 2, 8, D), F32),
+        pltpu.VMEM((PLANE // 2, 8, D), F32),
+        pltpu.VMEM((PLANE // 2, 8, D), F32),
+        pltpu.VMEM((PLANE // 2, 8, D), F32),
         pltpu.VMEM((NZ, 8, 128), F32),
         pltpu.VMEM((NZ, 8, 128), F32),
         pltpu.VMEM((2, 4, QD, D), BF16),
         pltpu.VMEM((2, 4, QD, D), BF16),
         *[pltpu.VMEM(result.shape, F32) for result in results],
-        sem((8,)), sem((8,)),
+        sem((13,)), sem((13,)),
         sem((2, 4, 2)), sem((2, 4, 2)),
         sem((2, 4, 2)), sem((2, 4, 2)),
         sem((4, NZ)), sem((4, NZ)),

time: 85.7 us -> 79.7 us (0.930); the launches traced: 84.6 us -> 79.6 us
  Pallas kernels: 84 us -> 78.9 us
    pallas_call x1, Pallas kernels: 81.8 us -> 76.8 us  [per_device(): pl.pallas_call(kernel, out_shape=results, in_specs=[hbm] * 8, out_specs=(...]
where the time goes in v2:
time: 79.7 us; the launch traced here: 79.6 us
  Pallas kernels  78.9 us (99%)
    pallas_call x1, Pallas kernels, per_device(): pl.pallas_call(kernel, out_shape=results, in_specs=[hbm] * 8, out_specs=(...  76.8 us
    pallas_call x1, Pallas kernels, per_device(): pl.pallas_call(place_outputs, out_shape=results, in_specs=[vmem] * 5, out...  2.12 us

profile of v2, /device:TPU:8, one launch (start us, length us, event | category | flops | bytes accessed | tf_op | source)
XLA Modules:
  0.0 79.6 jit_solution(10774804667942628571)
XLA Ops:
  0.6 76.8 %shard_map.119 = (f32[128,512]{1,0:T(8,128)}, f32[64,512]{1,0:T(8,128)}, f32[2,512]{1,0:T(2,128)}, f32[2,128,512]{2,1,0:T(8,128)}, f32[3,128]{1,0:T(4,128)}) custom-call(bf16[128,512]{1,0:T(8,128)(2,1)} %query_in.1, s32[4,128]{1,0:T(4,128)} %bitcast.4, s32[1,512]{1,0:T(1,128)} %bitcast.5, s32[1,128]{1,0:T(1,128)} %bitcast.6, s32[1,128]{1,0:T(1,128)} %bitcast.7, ...), custom_call_target="tpu_custom_call" | custom-call | tf_op jit(solution)/shard_map/pallas_call | solution.py:675
  77.4 2.1 %shard_map.120 = (f32[128,512]{1,0:T(8,128)}, f32[64,512]{1,0:T(8,128)}, f32[2,512]{1,0:T(2,128)}, f32[2,128,512]{2,1,0:T(8,128)}, f32[3,128]{1,0:T(4,128)}) custom-call(f32[128,512]{1,0:T(8,128)} %get-tuple-element.10.refs_0_, f32[64,512]{1,0:T(8,128)} %get-tuple-element.11.refs_1_, f32[2,512]{1,0:T(2,128)} %get-tuple-element.12.refs_2_, ...), custom_call_target="tpu_custom_call" | custom-call | tf_op jit(solution)/shard_map/pallas_call | solution.py:688

commit v3 on v2

--- a/solution.py
+++ b/solution.py
@@ -125,7 +125,7 @@
         pending.append(copy.wait_send)
 
     def flows(hop):
-        return [(0, 0), (1, 1), (1, 0), (0, 1)] if hop < 4 else [(0, 0), (1, 1)]
+        return [(0, 0), (1, 1), (0, 1), (1, 0)] if hop < 4 else [(0, 0), (1, 1)]
 
     for direction, chunk in flows(1):
         ag_start(direction, 1, chunk)
@@ -273,25 +273,21 @@
             o = ORDER[2 * t + o2]
             tstat[o : o + 1, :] = total[:, o2 * 128 : (o2 + 1) * 128]
 
-    def forward(hop, direction):
-        for chunk in range(2):
-            if hop < 4 or chunk == direction:
-                ag(direction, hop - 1, chunk).wait_recv()
-                ag_start(direction, hop, chunk)
-
-    for direction in range(2):
-        forward(2, direction)
+    def forward(hop):
+        for direction, chunk in flows(hop):
+            ag(direction, hop - 1, chunk).wait_recv()
+            ag_start(direction, hop, chunk)
+
+    forward(2)
     for d in range(1, NZ):
         tabcopy(d).wait_recv()
     pack(0)
-    for direction in range(2):
-        forward(3, direction)
+    forward(3)
     pack(1)
     for d in range(1, NX):
         wcopy(d, lax.rem(x - d + NX, NX)).wait_recv()
     top_scores(0)
-    for direction in range(2):
-        forward(4, direction)
+    forward(4)
     ag(1, 3, 0).wait_recv()
     pack(2)
     for load in loads[6:9]:
@@ -560,22 +556,11 @@
         arrived(f"ret{t}")
         part[t] = part[t] + dot(oht[t], pbk[t].reshape(SLOTS, D), NN)
 
+    send_losses()
     returned(3)
     rs_step(0, 0, 0)
     rs_step(1, 0, 1)
     rs_step(1, 1, 0)
-    returned(2)
-    rs_step(0, 1, 1)
-    rs_step(1, 1, 1)
-    rs_step(0, 1, 0)
-    rs_step(1, 2, 0)
-    send_losses()
-    rs_step(1, 2, 1)
-    returned(1)
-    rs_step(0, 2, 1)
-    rs_step(1, 3, 0)
-    rs_step(0, 2, 0)
-    rs_step(1, 3, 1)
     grads = jnp.zeros((272, D), F32)
     for t in range(STEPS):
         grads = grads + dot(deltas[t], rb[t].reshape(SLOTS, D), NN)
@@ -583,6 +568,17 @@
     mg_ref[...] = grads[256:258]
     store(0, lg_ref, lg_out)
     store(1, mg_ref, mg_out)
+    returned(2)
+    rs_step(0, 1, 1)
+    rs_step(1, 1, 1)
+    rs_step(0, 1, 0)
+    rs_step(1, 2, 0)
+    rs_step(1, 2, 1)
+    returned(1)
+    rs_step(0, 2, 1)
+    rs_step(1, 3, 0)
+    rs_step(0, 2, 0)
+    rs_step(1, 3, 1)
     returned(0)
     rs_step(0, 3, 1)
     rs_step(0, 3, 0)
@@ -665,7 +661,7 @@
         pltpu.VMEM((2, 4, QD, D), BF16),
         *[pltpu.VMEM(result.shape, F32) for result in results],
         sem((13,)), sem((13,)),
-        sem((2, 4, 2)), sem((2, 4, 2)),
+        sem((2, 4, 4)), sem((2, 4, 4)),
         sem((2, 4, 2)), sem((2, 4, 2)),
         sem((4, NZ)), sem((4, NZ)),
         sem((NX,)), sem((NX,)),

time: 79.7 us -> 78.2 us (0.981)
  Pallas kernels: 78.9 us -> 77.4 us
    pallas_call x1, Pallas kernels: 76.8 us -> 75.3 us  [per_device(): pl.pallas_call(kernel, out_shape=results, in_specs=[hbm] * 8, out_specs=(...]
where the time goes in v3:
time: 78.2 us; the launch traced here: 78.1 us
  Pallas kernels  77.4 us (99%)
    pallas_call x1, Pallas kernels, per_device(): pl.pallas_call(kernel, out_shape=results, in_specs=[hbm] * 8, out_specs=(...  75.3 us
    pallas_call x1, Pallas kernels, per_device(): pl.pallas_call(place_outputs, out_shape=results, in_specs=[vmem] * 5, out...  2.12 us

profile of v3, /device:TPU:8, one launch (start us, length us, event | category | flops | bytes accessed | tf_op | source)
XLA Modules:
  0.0 78.1 jit_solution(799065063696556376)
XLA Ops:
  0.6 75.3 %shard_map.119 = (f32[128,512]{1,0:T(8,128)}, f32[64,512]{1,0:T(8,128)}, f32[2,512]{1,0:T(2,128)}, f32[2,128,512]{2,1,0:T(8,128)}, f32[3,128]{1,0:T(4,128)}) custom-call(bf16[128,512]{1,0:T(8,128)(2,1)} %query_in.1, s32[4,128]{1,0:T(4,128)} %bitcast.4, s32[1,512]{1,0:T(1,128)} %bitcast.5, s32[1,128]{1,0:T(1,128)} %bitcast.6, s32[1,128]{1,0:T(1,128)} %bitcast.7, ...), custom_call_target="tpu_custom_call" | custom-call | tf_op jit(solution)/shard_map/pallas_call | solution.py:671
  75.9 2.1 %shard_map.120 = (f32[128,512]{1,0:T(8,128)}, f32[64,512]{1,0:T(8,128)}, f32[2,512]{1,0:T(2,128)}, f32[2,128,512]{2,1,0:T(8,128)}, f32[3,128]{1,0:T(4,128)}) custom-call(f32[128,512]{1,0:T(8,128)} %get-tuple-element.10.refs_0_, f32[64,512]{1,0:T(8,128)} %get-tuple-element.11.refs_1_, f32[2,512]{1,0:T(2,128)} %get-tuple-element.12.refs_2_, ...), custom_call_target="tpu_custom_call" | custom-call | tf_op jit(solution)/shard_map/pallas_call | solution.py:684

commit v4 on v3

--- a/solution.py
+++ b/solution.py
@@ -21,6 +21,8 @@
 ORDER = (0, 1, 7, 2, 6, 3, 5, 4)
 IDX = tuple(ORDER.index(o) for o in range(NZ))
 NEG = -1e30
+FAR_PLANE = sorted(range(1, PLANE), key=lambda i: -min(i // NDP, NX - i // NDP) - min(i % NDP, NDP - i % NDP) / 2)
+FAR_Z = (4, 3, 5, 2, 6, 1, 7)
 MESH = pl.DeviceIdType.MESH
 F32 = jnp.float32
 BF16 = jnp.bfloat16
@@ -163,7 +165,7 @@
 
     def send(name):
         phase, source, target = exchanges[name]
-        for i in range(1, PLANE):
+        for i in FAR_PLANE:
             remote(phase, source(*partner(i)), target.at[me], plane_id(i)).start()
         pending.append(whole(name).wait_send)
 
@@ -313,7 +315,7 @@
         )
 
     def share(slot, source, target):
-        for d in range(1, NZ):
+        for d in FAR_Z:
             zshare(slot, source, target, d).start()
             pending.append(zshare(slot, source, target, d).wait_send)
 

time: 78.2 us -> 76.2 us (0.974)
  Pallas kernels: 77.4 us -> 74.9 us
    pallas_call x1, Pallas kernels: 75.3 us -> 72.7 us  [per_device(): pl.pallas_call(kernel, out_shape=results, in_specs=[hbm] * 8, out_specs=(...]
where the time goes in v4:
time: 76.2 us; the launch traced here: 75.5 us
  Pallas kernels  74.9 us (98%)
    pallas_call x1, Pallas kernels, per_device(): pl.pallas_call(kernel, out_shape=results, in_specs=[hbm] * 8, out_specs=(...  72.7 us
    pallas_call x1, Pallas kernels, per_device(): pl.pallas_call(place_outputs, out_shape=results, in_specs=[vmem] * 5, out...  2.12 us

profile of v4, /device:TPU:8, one launch (start us, length us, event | category | flops | bytes accessed | tf_op | source)
XLA Modules:
  0.0 75.5 jit_solution(15092519418262192154)
XLA Ops:
  0.6 72.7 %shard_map.119 = (f32[128,512]{1,0:T(8,128)}, f32[64,512]{1,0:T(8,128)}, f32[2,512]{1,0:T(2,128)}, f32[2,128,512]{2,1,0:T(8,128)}, f32[3,128]{1,0:T(4,128)}) custom-call(bf16[128,512]{1,0:T(8,128)(2,1)} %query_in.1, s32[4,128]{1,0:T(4,128)} %bitcast.4, s32[1,512]{1,0:T(1,128)} %bitcast.5, s32[1,128]{1,0:T(1,128)} %bitcast.6, s32[1,128]{1,0:T(1,128)} %bitcast.7, ...), custom_call_target="tpu_custom_call" | custom-call | tf_op jit(solution)/shard_map/pallas_call | solution.py:673
  73.4 2.1 %shard_map.120 = (f32[128,512]{1,0:T(8,128)}, f32[64,512]{1,0:T(8,128)}, f32[2,512]{1,0:T(2,128)}, f32[2,128,512]{2,1,0:T(8,128)}, f32[3,128]{1,0:T(4,128)}) custom-call(f32[128,512]{1,0:T(8,128)} %get-tuple-element.10.refs_0_, f32[64,512]{1,0:T(8,128)} %get-tuple-element.11.refs_1_, f32[2,512]{1,0:T(2,128)} %get-tuple-element.12.refs_2_, ...), custom_call_target="tpu_custom_call" | custom-call | tf_op jit(solution)/shard_map/pallas_call | solution.py:686
